TPU v7x, 32 devices: a whole 2x2x4 slice. The times are simulated.
32 devices in a mesh: grp: 4 (over z), seq: 8 (over y, x, core).
Axes of the slice: x: 2, y: 2, z: 4, core: 2. Of those that a mesh axis runs over, the one named last changes fastest.
Arguments:
- tokens: bfloat16 [4096, 2048], P(('grp', 'seq')), may hold values from -6 to 6
- norm_gains: float32 [2, 2048], replicated, may hold values from 0.5 to 1.5
- norm_biases: float32 [2, 2048], replicated, may hold values from -1 to 1
- mix_weight: bfloat16 [2048, 3, 2048], P(None, None, 'seq'), may hold values from -0.125 to 0.125
- mix_bias: bfloat16 [3, 2048], P(None, 'seq'), may hold values from -1.796875 to 1.796875
- out_weight: bfloat16 [2048, 2048], P('seq'), may hold values from -0.5 to 0.5
- gate_up_weight: bfloat16 [2048, 2, 5632], P(None, None, 'seq'), may hold values from -0.125 to 0.125
- down_weight: bfloat16 [5632, 2048], P('seq'), may hold values from -0.078125 to 0.078125
- row_lengths: int32 [8], replicated, may hold values from 128 to 1024, as said below
- row_group: int32 [8], replicated, may hold values from 0 to 3, as said below
- cotangent: bfloat16 [4096, 2048], P(('grp', 'seq')), may hold values from -6 to 6
Outputs:
- layer_out: bfloat16 [4096, 2048], P(('grp', 'seq'))
- tokens_grad: bfloat16 [4096, 2048], P(('grp', 'seq'))
- gains_grad: float32 [2, 2048], replicated
- biases_grad: float32 [2, 2048], replicated
- mix_grad: float32 [2048, 3, 2048], P(None, None, 'seq')
- mix_bias_grad: float32 [3, 2048], P(None, 'seq')
- out_grad: float32 [2048, 2048], P('seq')
- gate_up_grad: float32 [2048, 2, 5632], P(None, None, 'seq')
- down_grad: float32 [5632, 2048], P('seq')
Inputs may be any that keep to these rules, and one draw needn't show every extreme that they name: `row_lengths`: rows 0 to 1 are 1024 long; every other row's length is a multiple of 128 and at most 256. `row_group`: each of rows 0 to 1 fills a group alone; every other group holds exactly three of the other rows.
All inputs are finite; a program needn't handle non-finite values.
Results may differ from a plain program's by a relative error of at most 0.02.
Values may be sent and summed in bfloat16 or wider, within the bound.
A program may use at most 320 MiB of HBM per device.

v0:
```python
import math

import jax
import jax.numpy as jnp
from jax import lax
from jax.sharding import PartitionSpec as P

HEAD_DIM = 64
ROT = 16


EPS = 1e-05
NEG = -1e30
BASE = 10000.0


def layer_norm(values, gain, bias):
    centered = values - jnp.mean(values, axis=-1, keepdims=True)
    scale = lax.rsqrt(jnp.mean(centered * centered, axis=-1, keepdims=True) + EPS)
    unit = centered * scale
    return (unit * gain + bias, unit, scale)


def norm_back(incoming, unit, scale, gain):
    along = incoming * gain
    inner = jnp.mean(along, axis=-1, keepdims=True)
    cross = jnp.mean(along * unit, axis=-1, keepdims=True)
    return (
        scale * (along - inner - unit * cross),
        jnp.sum(incoming * unit, axis=0),
        jnp.sum(incoming, axis=0),
    )


def rotate(values, where, sign):
    half = ROT // 2
    freq = BASE ** (-jnp.arange(half, dtype=jnp.float32) / half)
    angle = where.astype(jnp.float32)[:, None] * freq[None, :]
    cosine = jnp.cos(angle)[:, None, :]
    sine = sign * jnp.sin(angle)[:, None, :]
    first = values[..., :half]
    second = values[..., half:ROT]
    return jnp.concatenate(
        [first * cosine - second * sine, second * cosine + first * sine, values[..., ROT:]], axis=-1
    )


def unrotate(lowered, where):
    wide = lowered.astype(jnp.float32)
    turned = jnp.stack(
        [rotate(wide[:, 0], where, -1.0), rotate(wide[:, 1], where, -1.0), wide[:, 2]], axis=1
    )
    return turned.reshape(lowered.shape[0], 3, -1).astype(jnp.bfloat16)


def slot_rows(row_lengths, row_group, group, slots):
    order = jnp.arange(row_lengths.shape[0], dtype=jnp.int32)
    same = row_group == group
    earlier = (order[:, None] > order[None, :]) & same[None, :]
    begin = jnp.sum(jnp.where(earlier, row_lengths[None, :], 0), axis=1)
    finish = begin + row_lengths
    inside = same[None, :] & (slots[:, None] >= begin[None, :]) & (slots[:, None] < finish[None, :])
    label = jnp.sum(jnp.where(inside, order[None, :] + 1, 0), axis=1) - 1
    offset = jnp.sum(jnp.where(inside, slots[:, None] - begin[None, :], 0), axis=1)
    load = jnp.sum(jnp.where(same, row_lengths, 0))
    return (label, jnp.where(label < 0, slots - load, offset))


def block_scores(query, key, label, start, block):
    part = lax.dynamic_slice_in_dim(query, start, block, 0)
    rows = start + jnp.arange(block, dtype=jnp.int32)
    columns = jnp.arange(label.shape[0], dtype=jnp.int32)
    label_rows = lax.dynamic_slice_in_dim(label, start, block, 0)
    allowed = (label_rows[:, None] == label[None, :]) & (rows[:, None] >= columns[None, :])
    scores = jnp.einsum("qhe,khe->hqk", part, key, preferred_element_type=jnp.float32) * (
        1.0 / math.sqrt(query.shape[-1])
    )
    return (part, jnp.where(allowed[None], scores, NEG))


def attend(query, key, value, label, block):

    def one_block(index):
        part, scores = block_scores(query, key, label, index * block, block)
        top = jnp.max(scores, axis=-1, keepdims=True)
        weights = jnp.exp(scores - top)
        totals = jnp.sum(weights, axis=-1, keepdims=True)
        probs = (weights / totals).astype(jnp.bfloat16)
        mixed = jnp.einsum("hqk,khe->qhe", probs, value, preferred_element_type=jnp.float32)
        return (mixed, top[..., 0] + jnp.log(totals[..., 0]))

    mixed, log_totals = lax.map(one_block, jnp.arange(query.shape[0] // block, dtype=jnp.int32))
    return (mixed.reshape(query.shape), log_totals)


def attend_back(query, key, value, label, log_totals, mixed_back, block):
    scale = 1.0 / math.sqrt(query.shape[-1])

    def one_block(carry, index):
        key_back, value_back = carry
        start = index * block
        part, scores = block_scores(query, key, label, start, block)
        back_part = lax.dynamic_slice_in_dim(mixed_back, start, block, 0)
        probs = jnp.exp(scores - log_totals[index][..., None])
        value_back = value_back + jnp.einsum(
            "hqk,qhe->khe",
            probs.astype(jnp.bfloat16),
            back_part,
            preferred_element_type=jnp.float32,
        )
        probs_back = jnp.einsum(
            "qhe,khe->hqk", back_part, value, preferred_element_type=jnp.float32
        )
        inner = jnp.sum(probs_back * probs, axis=-1, keepdims=True)
        score_back = (probs * (probs_back - inner)).astype(jnp.bfloat16)
        query_back = (
            jnp.einsum("hqk,khe->qhe", score_back, key, preferred_element_type=jnp.float32) * scale
        )
        key_back = (
            key_back
            + jnp.einsum("hqk,qhe->khe", score_back, part, preferred_element_type=jnp.float32)
            * scale
        )
        return ((key_back, value_back), query_back)

    empty = jnp.zeros(key.shape, jnp.float32)
    (key_back, value_back), query_back = lax.scan(
        one_block, (empty, empty), jnp.arange(query.shape[0] // block, dtype=jnp.int32)
    )
    return (query_back.reshape(query.shape), key_back, value_back)


def silu_parts(gate_up):
    gate = gate_up[:, 0]
    upper = gate_up[:, 1]
    sigma = jax.nn.sigmoid(gate)
    return (gate * sigma * upper, gate, upper, sigma)


def gate_back(hidden_back, gate, upper, sigma):
    gate_part = hidden_back * upper * sigma * (1.0 + gate * (1.0 - sigma))
    up_part = hidden_back * gate * sigma
    return jnp.stack([gate_part, up_part], axis=1).astype(jnp.bfloat16)


def gather_rows(values):
    return lax.all_gather(values, "seq", axis=0, tiled=True)


def summed_rows(product, left):
    return lax.psum_scatter(
        product(left).astype(jnp.bfloat16), "seq", scatter_dimension=0, tiled=True
    ).astype(jnp.float32)


def on_device(
    tokens,
    norm_gains,
    norm_biases,
    mix_weight,
    mix_bias,
    out_weight,
    gate_up_weight,
    down_weight,
    row_lengths,
    row_group,
    cotangent,
):
    seq_count = lax.axis_size("seq")
    shard = lax.axis_index("seq")
    group = lax.axis_index("grp")
    slots_dev = tokens.shape[0]
    width = tokens.shape[1]
    group_slots = slots_dev * seq_count
    block = min(512, group_slots)
    local_width = width // seq_count
    local_heads = local_width // HEAD_DIM
    mine = shard * slots_dev + jnp.arange(slots_dev, dtype=jnp.int32)
    label_mine, place_mine = slot_rows(row_lengths, row_group, group, mine)
    label_all, place_all = slot_rows(
        row_lengths, row_group, group, jnp.arange(group_slots, dtype=jnp.int32)
    )
    inputs = tokens.astype(jnp.float32)
    upstream = cotangent.astype(jnp.float32) * (label_mine >= 0).astype(jnp.float32)[:, None]
    upstream_low = upstream.astype(jnp.bfloat16)
    normed, unit_one, scale_one = layer_norm(inputs, norm_gains[0], norm_biases[0])
    normed_low = normed.astype(jnp.bfloat16)
    mix_full, bias_full, out_full = (
        lax.all_gather(mix_weight, "seq", axis=2, tiled=True),
        lax.all_gather(mix_bias, "seq", axis=1, tiled=True),
        lax.all_gather(out_weight, "seq", axis=0, tiled=True),
    )
    mixin = jnp.einsum(
        "td,dcf->tcf", normed_low, mix_full, preferred_element_type=jnp.float32
    ) + bias_full.astype(jnp.float32)
    heads_in = mixin.reshape(slots_dev, 3, width // HEAD_DIM, HEAD_DIM)
    sending = jnp.stack(
        [
            rotate(heads_in[:, 0], place_mine, 1.0),
            rotate(heads_in[:, 1], place_mine, 1.0),
            heads_in[:, 2],
        ],
        axis=1,
    ).astype(jnp.bfloat16)
    arrived = lax.all_to_all(
        sending.reshape(slots_dev, 3, seq_count, local_width),
        "seq",
        split_axis=2,
        concat_axis=0,
        tiled=True,
    )
    arrived = arrived.reshape(group_slots, 3, local_heads, HEAD_DIM)
    query, key, value = (arrived[:, 0], arrived[:, 1], arrived[:, 2])
    mixed, log_totals = attend(query, key, value, label_all, block)
    attended = lax.all_to_all(
        mixed.reshape(group_slots, local_width).astype(jnp.bfloat16),
        "seq",
        split_axis=0,
        concat_axis=1,
        tiled=True,
    )
    resid = inputs + jnp.dot(attended, out_full, preferred_element_type=jnp.float32)
    normed_two, unit_two, scale_two = layer_norm(resid, norm_gains[1], norm_biases[1])
    normed_two_all = gather_rows(normed_two.astype(jnp.bfloat16))
    gate_up = jnp.einsum(
        "td,dcf->tcf", normed_two_all, gate_up_weight, preferred_element_type=jnp.float32
    )
    hidden, gate, upper, sigma = silu_parts(gate_up)
    hidden_low = hidden.astype(jnp.bfloat16)

    def down_product(part):
        return jnp.dot(part, down_weight, preferred_element_type=jnp.float32)

    layer_out = resid + summed_rows(down_product, hidden_low)
    upstream_all = gather_rows(upstream_low)
    down_shard = jnp.einsum(
        "tf,td->fd", hidden_low, upstream_all, preferred_element_type=jnp.float32
    )
    hidden_back = jnp.einsum(
        "td,fd->tf", upstream_all, down_weight, preferred_element_type=jnp.float32
    )
    gate_up_back = gate_back(hidden_back, gate, upper, sigma)
    gate_up_shard = jnp.einsum(
        "td,tcf->dcf", normed_two_all, gate_up_back, preferred_element_type=jnp.float32
    )

    def gate_up_product(part):
        return jnp.einsum("tcf,dcf->td", part, gate_up_weight, preferred_element_type=jnp.float32)

    normed_two_back = summed_rows(gate_up_product, gate_up_back)
    resid_part, gain_two, bias_two = norm_back(normed_two_back, unit_two, scale_two, norm_gains[1])
    resid_back = upstream + resid_part
    branch_low = resid_back.astype(jnp.bfloat16)
    out_term = jnp.einsum("te,td->ed", attended, branch_low, preferred_element_type=jnp.float32)
    attended_back = jnp.einsum(
        "td,ed->te", branch_low, out_full, preferred_element_type=jnp.float32
    ).astype(jnp.bfloat16)
    heads_back = lax.all_to_all(
        attended_back, "seq", split_axis=1, concat_axis=0, tiled=True
    ).reshape(group_slots, local_heads, HEAD_DIM)
    query_back, key_back, value_back = attend_back(
        query, key, value, label_all, log_totals, heads_back, block
    )
    lowered = (
        jnp.stack([query_back, key_back, value_back], axis=1)
        .astype(jnp.bfloat16)
        .reshape(group_slots, 3, 1, local_width)
    )
    returned = lax.all_to_all(lowered, "seq", split_axis=0, concat_axis=2, tiled=True).reshape(
        slots_dev, 3, width // HEAD_DIM, HEAD_DIM
    )
    mixin_back = unrotate(returned, place_mine)
    mix_term = jnp.einsum("td,tcf->dcf", normed_low, mixin_back, preferred_element_type=jnp.float32)
    bias_term = jnp.sum(mixin_back, axis=0, dtype=jnp.float32)
    normed_back = jnp.einsum(
        "tcf,dcf->td", mixin_back, mix_full, preferred_element_type=jnp.float32
    )
    mix_shard, bias_shard, out_shard = (
        lax.psum_scatter(
            mix_term.astype(jnp.bfloat16), "seq", scatter_dimension=2, tiled=True
        ).astype(jnp.float32),
        lax.psum_scatter(
            bias_term.astype(jnp.bfloat16), "seq", scatter_dimension=1, tiled=True
        ).astype(jnp.float32),
        lax.psum_scatter(
            out_term.astype(jnp.bfloat16), "seq", scatter_dimension=0, tiled=True
        ).astype(jnp.float32),
    )
    tokens_part, gain_one, bias_one = norm_back(normed_back, unit_one, scale_one, norm_gains[0])
    tokens_grad = (resid_back + tokens_part).astype(jnp.bfloat16)
    mix_grad, mix_bias_grad, out_grad, gate_up_grad, down_grad = (
        lax.psum(mix_shard.astype(jnp.bfloat16), "grp").astype(jnp.float32),
        lax.psum(bias_shard.astype(jnp.bfloat16), "grp").astype(jnp.float32),
        lax.psum(out_shard.astype(jnp.bfloat16), "grp").astype(jnp.float32),
        lax.psum(gate_up_shard.astype(jnp.bfloat16), "grp").astype(jnp.float32),
        lax.psum(down_shard.astype(jnp.bfloat16), "grp").astype(jnp.float32),
    )
    gains_grad, biases_grad = lax.psum(
        (jnp.stack([gain_one, gain_two]), jnp.stack([bias_one, bias_two])), ("grp", "seq")
    )
    return (
        layer_out.astype(jnp.bfloat16),
        tokens_grad,
        gains_grad,
        biases_grad,
        mix_grad,
        mix_bias_grad,
        out_grad,
        gate_up_grad,
        down_grad,
    )


def solution(mesh):
    placed = (
        P(("grp", "seq"), None),
        P(),
        P(),
        P(None, None, "seq"),
        P(None, "seq"),
        P("seq", None),
        P(None, None, "seq"),
        P("seq", None),
        P(),
        P(),
        P(("grp", "seq"), None),
    )
    return jax.shard_map(
        on_device,
        mesh=mesh,
        in_specs=placed,
        out_specs=(
            P(("grp", "seq"), None),
            P(("grp", "seq"), None),
            P(),
            P(),
            P(None, None, "seq"),
            P(None, "seq"),
            P("seq", None),
            P(None, None, "seq"),
            P("seq", None),
        ),
        check_vma=False,
    )
```

profile of v0, /device:TPU:0, one launch (start us, length us, event | category | flops | bytes accessed | tf_op | source)
XLA Modules:
  0.0 1248.3 jit_solution(738130817734868844)
XLA Ops:
  9.5 10.4 all_gather.16
  21.9 121.0 %all-gather.5.cloned.1.call-done = bf16[2048,3,2048]{2,0,1:T(8,128)(2,1)} async-done(((bf16[2048,3,256]{2,0,1:T(8,128)(2,1)}), bf16[2048,3,2048]{2,0,1:T(8,128)(2,1)}) %all-gather.5.cloned.1.call-update) | async-done | bytes 25165840 | tf_op jit(solution)/shard_map/all_gather | solution.py:189
  143.0 13.4 %convolution_add_fusion = f32[128,3,2048]{2,0,1:T(8,128)} fusion(bf16[2048,3,2048]{2,0,1:T(8,128)(2,1)} %all-gather.5.cloned.1.call-done, f32[3,2048]{1,0:T(4,128)S(1)} %convert_element_type.139, bf16[128,2048]{1,0:T(8,128)(2,1)S(1)} %copy-done.5, f32[2048]{0:T(1024)S(1)} %bitcast.195, f32[2048]{0:T(1024)S(1)} %bitcast.191, f32[128]{0:T(128)S(1)} %add_rsqrt_fusion.1, ...), kind=kOutput, calls=%fused_computation.63 | convolution fusion | flops 3223584768 | bytes 28877824 | tf_op jit(solution)/shard_map/td,dcf->tcf/dot_general | solution.py:193
  156.4 3.5 copy.90
  164.7 4.5 all-to-all-start
  169.3 35.6 %all-to-all-done = bf16[128,3,8,256]{0,3,1,2:T(8,128)(2,1)} async-done(((bf16[128,3,8,256]{0,3,1,2:T(8,128)(2,1)}), bf16[128,3,8,256]{0,3,1,2:T(8,128)(2,1)}, u32[]{:S(2)}, u32[]{:S(2)}) %all-to-all-start) | async-done | bytes 1572896 | tf_op jit(solution)/shard_map/all_to_all | solution.py:205
  204.9 3.6 copy.92
  208.5 3.7 reshape.381
  212.2 2.6 slice_bitcast_fusion.6
  215.6 21.5 %while.27 = (s32[]{:T(128)}, bf16[2,512,4,64]{1,3,2,0:T(8,128)(2,1)}, f32[2,4,512]{2,1,0:T(4,128)S(1)}, s32[2]{0:T(128)S(1)}, s32[1024]{0:T(1024)S(1)}, /*index=...) while((s32[]{:T(128)}, ...), condition=%wide.region_10.11_spmd, body=%wide.region_7.10_spmd.sunk | while | flops 563608064 | bytes 35469596 | solution.py:92
  217.5 2.6 fusion.126
  220.1 2.3 fusion.127
  222.5 3.0 fusion.128
  228.2 2.6 fusion.126
  230.9 2.3 fusion.127
  233.3 3.0 fusion.128
  237.1 2.4 copy.93
  239.5 2.2 convert_element_type.142
  241.6 1.9 copy.94
  243.5 4.2 all-to-all-start.1
  247.8 9.7 all-to-all-done.1
  257.4 4.9 fusion.81
  264.5 2.0 fusion.66
  266.9 33.4 %all-gather.9.cloned.1.call-done = bf16[1024,2048]{1,0:T(8,128)(2,1)} async-done(((bf16[128,2048]{1,0:T(8,128)(2,1)}), bf16[1024,2048]{1,0:T(8,128)(2,1)}) %all-gather.9.cloned.1.call-update) | async-done | bytes 4194320 | tf_op jit(solution)/shard_map/all_gather | solution.py:147
  300.4 11.0 fusion.39
  311.4 28.1 %all-gather.11.cloned.1.call-done = bf16[1024,2048]{1,0:T(8,128)(2,1)} async-done(((bf16[128,2048]{1,0:T(8,128)(2,1)}), bf16[1024,2048]{1,0:T(8,128)(2,1)}) %all-gather.11.cloned.1.call-update) | async-done | bytes 4194320 | tf_op jit(solution)/shard_map/all_gather | solution.py:147
  339.5 8.3 fusion.45
  349.4 11.0 bitcast_convert_fusion
  360.4 6.4 convolution_convert_fusion.3
  366.9 45.0 %reduce-scatter.10.cloned.1.call-done = bf16[128,2048]{1,0:T(8,128)(2,1)} async-done(((bf16[1024,2048]{1,0:T(8,128)(2,1)}), bf16[128,2048]{1,0:T(8,128)(2,1)}) %reduce-scatter.10.cloned.1.call-update) | async-done | bytes 524304 | tf_op jit(solution)/shard_map/reduce_scatter | solution.py:151
  411.9 2.1 fusion.65
  414.0 53.4 %reduce-scatter.8.cloned.1.call-done = bf16[128,2048]{1,0:T(8,128)(2,1)} async-done(((bf16[1024,2048]{1,0:T(8,128)(2,1)}), bf16[128,2048]{1,0:T(8,128)(2,1)}) %reduce-scatter.8.cloned.1.call-update) | async-done | bytes 524304 | tf_op jit(solution)/shard_map/reduce_scatter | solution.py:151
  467.3 2.3 fusion.63
  469.7 7.1 convolution_convert_fusion.1
  476.8 6.3 convolution_convert_fusion.5
  484.0 3.5 all-to-all-start.2
  487.7 9.4 all-to-all-done.2
  498.2 2.1 reshape.382
  501.1 31.6 %while.28 = (s32[]{:T(128)}, f32[1024,4,64]{0,2,1:T(8,128)S(1)}, f32[1024,4,64]{0,2,1:T(8,128)}, bf16[2,512,4,64]{1,3,2,0:T(8,128)(2,1)}, s32[2]{0:T(128)S(1)}, ...) while((s32[]{:T(128)}, f32[1024,4,64]{0,2,1:T(8,128)S(1)}, ...), condition=%wide.region_19.20_spmd.clone, body=%wide.region_17.19_spmd.clone.sunk | while | flops 1376647680 | bytes 87103920 | solution.py:127
  506.4 2.5 fusion.141
  508.9 3.2 multiply_reduce_fusion.4
  512.1 2.4 multiply_convert_fusion.5
  522.2 2.6 fusion.141
  524.7 3.2 multiply_reduce_fusion.4
  527.9 2.4 multiply_convert_fusion.5
  532.8 1.7 copy.97
  537.6 3.0 copy.98
  540.5 29.5 %all_to_all.56 = bf16[1024,3,1,256]{3,1,2,0:T(4,128)(2,1)S(1)} all-to-all(bf16[1024,3,1,256]{3,1,2,0:T(4,128)(2,1)S(1)} %copy.98), channel_id=1, replica_groups=mesh['grp'=4,'seq'=8] {'seq'}, dimensions={0} | all-to-all | bytes 3145728 | tf_op jit(solution)/shard_map/all_to_all | solution.py:269
  571.4 1.9 copy.100
  573.4 2.1 convert_element_type.158
  575.7 1.7 slice_bitcast_fusion.3
  578.5 12.0 convolution_convert_fusion
  590.6 10.8 convolution_convert_fusion.2
  603.1 8.9 convolution_convert_fusion.4
  612.0 134.7 %reduce-scatter.12.cloned.1.call-done = bf16[2048,3,256]{2,0,1:T(8,128)(2,1)} async-done(((bf16[2048,3,2048]{2,0,1:T(8,128)(2,1)}), bf16[2048,3,256]{2,0,1:T(8,128)(2,1)}) %reduce-scatter.12.cloned.1.call-update) | async-done | bytes 3145744 | tf_op jit(solution)/shard_map/reduce_scatter | solution.py:279
  746.7 14.6 %fusion.59 = (f32[2048]{0:T(1024)S(1)}, f32[128]{0:T(128)S(1)}, f32[128]{0:T(128)S(1)}, f32[2048]{0:T(1024)S(1)}, f32[128,2048]{1,0:T(8,128)}) fusion(bf16[128,2048]{1,0:T(8,128)(2,1)S(1)} %copy-done.6, f32[128]{0:T(128)S(1)} %copy-done.35, f32[128]{0:T(128)S(1)} %copy-done.33, f32[2048]{0:T(1024)S(1)} %bitcast.193, ...), kind=kOutput, calls=%fused_computation.93 | convolution fusion | flops 3225415680 | bytes 28338176 | tf_op jit(solution)/shard_map/tcf,dcf->td/dot_general | solution.py:275
  761.4 40.2 %all-reduce = (f32[2,2048]{1,0:T(2,128)}, f32[2,2048]{1,0:T(2,128)}) all-reduce(f32[2,2048]{1,0:T(2,128)S(1)} %pad_maximum_fusion.10, f32[2,2048]{1,0:T(2,128)S(1)} %pad_maximum_fusion.11), channel_id=1, replica_groups=mesh['grp'=4,'seq'=8] {'grp','seq'}, use_global_device_ids=true, to_apply=%region_24.25 | all-reduce | flops 8192 | bytes 65536 | tf_op jit(solution)/shard_map/psum | solution.py:298
  801.6 2.5 fusion.58
  805.0 12.3 psum.52
  817.9 407.1 %all-reduce.4.cloned.1.call-done = (bf16[2048,3,256]{2,0,1:T(8,128)(2,1)}, bf16[256,2048]{1,0:T(8,128)(2,1)}, bf16[2048,2,704]{0,2,1:T(8,128)(2,1)}, bf16[704,2048]{1,0:T(8,128)(2,1)}) async-done(((bf16[2048,3,256]{2,0,1:T(8,128)(2,1)}, bf16[256,2048]{1,0:T(8,128)(2,1)}, bf16[2048,2,704]{0,2,1:T(8,128)(2,1)}, bf16[704,2048]{1,0:T(8,128)(2,1)}), (bf16[2048,3,256]{2,0,1:T(8,128)(2,1)}, ...) | async-done | bytes 12845072 | tf_op jit(solution)/shard_map/psum | solution.py:292
  1225.0 2.9 convert_element_type.164
  1228.0 3.7 convert_element_type.161
  1231.7 3.3 convert_element_type.168
  1235.0 6.0 convert_element_type.166
  (216 shorter events, 40.4 us)
Async XLA Ops:
  7.2 332.3 %copy-start = (bf16[704,2048]{1,0:T(8,128)(2,1)S(1)}, bf16[704,2048]{1,0:T(8,128)(2,1)}, u32[]{:S(2)}) copy-start(bf16[704,2048]{1,0:T(8,128)(2,1)} %param.22) | copy-start | bytes 8650756
  7.2 1.6 copy-start.38
  7.2 1.6 copy-start.37
  7.2 2.3 copy-start.36
  7.2 12.8 %copy-start.5 = (bf16[128,2048]{1,0:T(8,128)(2,1)S(1)}, bf16[128,2048]{1,0:T(8,128)(2,1)}, u32[]{:S(2)}) copy-start(bf16[128,2048]{1,0:T(8,128)(2,1)} %param.15) | copy-start | bytes 1572868
  7.2 14.6 %copy-start.30 = (f32[2,2048]{1,0:T(2,128)S(1)}, f32[2,2048]{1,0:T(2,128)}, u32[]{:S(2)}) copy-start(f32[2,2048]{1,0:T(2,128)} %param.16) | copy-start | bytes 49156
  7.2 14.6 %copy-start.31 = (f32[2,2048]{1,0:T(2,128)S(1)}, f32[2,2048]{1,0:T(2,128)}, u32[]{:S(2)}) copy-start(f32[2,2048]{1,0:T(2,128)} %param.17) | copy-start | bytes 49156
  7.3 135.7 %all-gather.5.cloned.1.call-start = ((), (), s32[]{:S(2)}) async-start(), calls=%async_computation.9 | async-start | bytes 28311552 | tf_op jit(solution)/shard_map/all_gather | solution.py:189
  8.0 239.8 %all-gather.7.cloned.1.call-start = ((), (), s32[]{:S(2)}) async-start(), calls=%async_computation.10 | async-start | bytes 9437184 | tf_op jit(solution)/shard_map/all_gather | solution.py:191
  20.2 136.2 %copy-start.32 = (f32[128]{0:T(128)}, f32[128]{0:T(128)S(1)}, u32[]{:S(2)}) copy-start(f32[128]{0:T(128)S(1)} %broadcast_multiply_fusion.6) | copy-start | bytes 1540
  20.5 135.9 %copy-start.34 = (f32[128]{0:T(128)}, f32[128]{0:T(128)S(1)}, u32[]{:S(2)}) copy-start(f32[128]{0:T(128)S(1)} %add_rsqrt_fusion.1) | copy-start | bytes 1540
  21.9 141.2 %copy-start.25 = (f32[128,8]{0,1:T(8,128)}, f32[128,8]{0,1:T(8,128)S(1)}, u32[]{:S(2)}) copy-start(f32[128,8]{0,1:T(8,128)S(1)} %get-tuple-element.253) | copy-start | bytes 12292
  21.9 134.5 %copy-start.21 = (f32[1,2048]{1,0:T(1,128)}, f32[1,2048]{1,0:T(1,128)S(1)}, u32[]{:S(2)}) copy-start(f32[1,2048]{1,0:T(1,128)S(1)} %get-tuple-element.244) | copy-start | bytes 24580
  21.9 134.4 %copy-start.23 = (f32[1,2048]{1,0:T(1,128)}, f32[1,2048]{1,0:T(1,128)S(1)}, u32[]{:S(2)}) copy-start(f32[1,2048]{1,0:T(1,128)S(1)} %get-tuple-element.246) | copy-start | bytes 24580
  164.7 40.2 %all-to-all-start = ((bf16[128,3,8,256]{0,3,1,2:T(8,128)(2,1)}), bf16[128,3,8,256]{0,3,1,2:T(8,128)(2,1)}, u32[]{:S(2)}, u32[]{:S(2)}) async-start(bf16[128,3,8,256]{0,3,1,2:T(8,128)(2,1)} %copy.91), calls=%async_computation | async-start | bytes 3145728 | tf_op jit(solution)/shard_map/all_to_all | solution.py:205
  220.1 2.4 copy-start.7
  220.1 2.4 copy-start.16
  225.5 0.8 copy-start.17
  230.9 2.4 copy-start.7
  230.9 2.4 copy-start.16
  236.3 0.8 copy-start.17
  243.5 13.9 %all-to-all-start.1 = ((bf16[8,128,256]{1,2,0:T(8,128)(2,1)}), bf16[8,128,256]{1,2,0:T(8,128)(2,1)}, u32[]{:S(2)}, u32[]{:S(2)}) async-start(bf16[8,128,256]{1,2,0:T(8,128)(2,1)} %copy.94), calls=%async_computation.1 | async-start | bytes 1048576 | tf_op jit(solution)/shard_map/all_to_all | solution.py:215
  247.7 52.7 %all-gather.9.cloned.1.call-start = ((), (), s32[]{:S(2)}) async-start(), calls=%async_computation.11 | async-start | bytes 4718592 | tf_op jit(solution)/shard_map/all_gather | solution.py:147
  262.4 1.0 copy-start.3
  264.4 75.0 %all-gather.11.cloned.1.call-start = ((), (), s32[]{:S(2)}) async-start(), calls=%async_computation.13 | async-start | bytes 4718592 | tf_op jit(solution)/shard_map/all_gather | solution.py:147
  266.5 145.4 %reduce-scatter.10.cloned.1.call-start = ((), (), s32[]{:S(2)}) async-start(), calls=%async_computation.14 | async-start | bytes 4718592 | tf_op jit(solution)/shard_map/reduce_scatter | solution.py:151
  347.8 1.1 copy-start.39
  347.8 1.6 copy-start.40
  360.4 107.0 %reduce-scatter.8.cloned.1.call-start = ((), (), s32[]{:S(2)}) async-start(), calls=%async_computation.12 | async-start | bytes 4718592 | tf_op jit(solution)/shard_map/reduce_scatter | solution.py:151
  366.8 45.0 %copy-start.4 = (f32[128,2048]{1,0:T(8,128)S(1)}, f32[128,2048]{1,0:T(8,128)}, u32[]{:S(2)}) copy-start(f32[128,2048]{1,0:T(8,128)} %copy-done.3) | copy-start | bytes 3145732
  366.8 100.5 %copy-start.18 = (bf16[128,2048]{1,0:T(8,128)(2,1)S(1)}, bf16[128,2048]{1,0:T(8,128)(2,1)}, u32[]{:S(2)}) copy-start(bf16[128,2048]{1,0:T(8,128)(2,1)} %param.25) | copy-start | bytes 1572868
  366.9 245.1 %reduce-scatter.14.cloned.1.call-start = ((), (), s32[]{:S(2)}) async-start(), calls=%async_computation.16 | async-start | bytes 9437184 | tf_op jit(solution)/shard_map/reduce_scatter | solution.py:285
  469.7 7.2 copy-start.9
  483.1 18.0 %copy-start.2 = (bf16[1024,4,64]{0,2,1:T(8,128)(2,1)S(1)}, bf16[1024,4,64]{0,2,1:T(8,128)(2,1)}, u32[]{:S(2)}) copy-start(bf16[1024,4,64]{0,2,1:T(8,128)(2,1)} %get-tuple-element.490) | copy-start | bytes 1572868
  483.1 18.0 %copy-start.8 = (bf16[1024,4,64]{0,2,1:T(8,128)(2,1)S(1)}, bf16[1024,4,64]{0,2,1:T(8,128)(2,1)}, u32[]{:S(2)}) copy-start(bf16[1024,4,64]{0,2,1:T(8,128)(2,1)} %get-tuple-element.491) | copy-start | bytes 1572868
  484.0 13.2 %all-to-all-start.2 = ((bf16[128,8,256]{2,0,1:T(8,128)(2,1)}), bf16[128,8,256]{2,0,1:T(8,128)(2,1)S(1)}, u32[]{:S(2)}, u32[]{:S(2)}) async-start(bf16[128,8,256]{2,0,1:T(8,128)(2,1)} %bitcast.142), calls=%async_computation.4 | async-start | bytes 1048576 | tf_op jit(solution)/shard_map/all_to_all | solution.py:258
  487.5 259.2 %reduce-scatter.12.cloned.1.call-start = ((), (), s32[]{:S(2)}) async-start(), calls=%async_computation.15 | async-start | bytes 28311552 | tf_op jit(solution)/shard_map/reduce_scatter | solution.py:279
  505.0 1.3 copy-start.11
  505.0 1.4 copy-start.19
  508.9 3.2 copy-start.20
  512.1 2.4 copy-start.14
  515.9 1.0 copy-start.15
  520.8 1.3 copy-start.11
  520.8 1.4 copy-start.19
  524.7 3.2 copy-start.20
  527.9 2.4 copy-start.14
  531.7 1.0 copy-start.15
  575.4 2.1 copy-start.26
  575.4 2.1 copy-start.29
  577.4 1.0 copy-start.6
  577.4 1.0 copy-start.22
  577.4 1.0 copy-start.24
  577.4 1.0 copy-start.33
  577.4 1.0 copy-start.35
  590.5 213.5 %reduce-scatter.16.cloned.1.call-start = ((), (), s32[]{:S(2)}) async-start(), calls=%async_computation.17 | async-start | bytes 589824
  602.8 622.3 %all-reduce.4.cloned.1.call-start = ((), (), s32[]{:S(2)}) async-start(), calls=%async_computation.18 | async-start | bytes 25690112 | tf_op jit(solution)/shard_map/psum | solution.py:292
  746.7 14.7 %copy-start.28 = (f32[2048]{0:T(1024)S(1)}, f32[2048]{0:T(1024)}, u32[]{:S(2)}) copy-start(f32[2048]{0:T(1024)} %get-tuple-element.165) | copy-start | bytes 24580
  746.7 14.7 %copy-start.27 = (f32[2048]{0:T(1024)S(1)}, f32[2048]{0:T(1024)}, u32[]{:S(2)}) copy-start(f32[2048]{0:T(1024)} %get-tuple-element.170) | copy-start | bytes 24580
  746.7 54.9 %copy-start.10 = (f32[128,2048]{1,0:T(8,128)S(1)}, f32[128,2048]{1,0:T(8,128)}, u32[]{:S(2)}) copy-start(f32[128,2048]{1,0:T(8,128)} %copy-done.9) | copy-start | bytes 3145732
  1225.0 2.9 copy-start.12
  1225.0 10.0 slice-start
  1228.0 3.7 copy-start.13
  1228.0 7.1 slice-start.1
  1235.0 6.0 copy-start.1
Sparse Core Ops, SparseCore 0:
  10.0 132.9 all-gather.4
  144.9 68.7 all-gather.6
  264.5 35.7 all-gather.8
  302.7 36.7 all-gather.10
  360.5 51.3 reduce-scatter.9
  416.0 51.2 reduce-scatter.7
  476.9 71.4 reduce-scatter.13
  590.6 155.9 reduce-scatter.11
  750.0 34.2 reduce-scatter.15
  788.2 436.8 all-reduce.3
where the time goes:
time: 1250 us
  waiting for transfers between devices  879 us (70%)
  matrix products  145 us (12%)
  blocking collectives  92.4 us (7%)
  local copies, waits for them, and re-layouts  49.7 us (4%)
  other arithmetic  47.1 us (4%)
  between operations  15.2 us (1%)
  starting transfers between devices  13.4 us (1%)
    psum x1, waiting for transfers between devices, on_device(): lax.psum(mix_shard.astype(jnp.bfloat16), 'grp').astype(jnp.float32)  407 us
    reduce_scatter x1, waiting for transfers between devices, on_device(): lax.psum_scatter(mix_term.astype(jnp.bfloat16), 'seq', scatter_dimension=...  135 us
    all_gather x1, waiting for transfers between devices, on_device(): lax.all_gather(mix_weight, 'seq', axis=2, tiled=True)  121 us
    reduce_scatter x2, waiting for transfers between devices, summed_rows(): lax.psum_scatter(product(left).astype(jnp.bfloat16), 'seq', scatter_dimen...  98.3 us
    all_gather x2, waiting for transfers between devices, gather_rows(): return lax.all_gather(values, 'seq', axis=0, tiled=True)  61.5 us
    psum x1, blocking collectives, on_device(): lax.psum((jnp.stack([gain_one, gain_two]), jnp.stack([bias_one, bias_two]...  40.2 us
    all_to_all x1, waiting for transfers between devices, on_device(): lax.all_to_all(sending.reshape(slots_dev, 3, seq_count, local_width), 'se...  35.6 us
    all_to_all x1, blocking collectives, on_device(): lax.all_to_all(lowered, 'seq', split_axis=0, concat_axis=2, tiled=True)  29.5 us
  transfers between devices with their start and end apart: 13, of which 10 were waited for; matrix products, arithmetic and copies ran while one was open for 15% of the time, Pallas kernels for 0%

commit v1 on v0

--- a/solution.py
+++ b/solution.py
@@ -1,8 +1,11 @@
+import functools
 import math
 
 import jax
 import jax.numpy as jnp
 from jax import lax
+from jax.experimental import pallas as pl
+from jax.experimental.pallas import tpu as pltpu
 from jax.sharding import PartitionSpec as P
 
 HEAD_DIM = 64
@@ -153,7 +156,7 @@
     ).astype(jnp.float32)
 
 
-def on_device(
+def plain_device(
     tokens,
     norm_gains,
     norm_biases,
@@ -184,117 +187,75 @@
     upstream = cotangent.astype(jnp.float32) * (label_mine >= 0).astype(jnp.float32)[:, None]
     upstream_low = upstream.astype(jnp.bfloat16)
     normed, unit_one, scale_one = layer_norm(inputs, norm_gains[0], norm_biases[0])
-    normed_low = normed.astype(jnp.bfloat16)
-    mix_full, bias_full, out_full = (
-        lax.all_gather(mix_weight, "seq", axis=2, tiled=True),
-        lax.all_gather(mix_bias, "seq", axis=1, tiled=True),
-        lax.all_gather(out_weight, "seq", axis=0, tiled=True),
-    )
+    normed_all = gather_rows(normed.astype(jnp.bfloat16))
+    up_four = lax.all_gather(upstream_low, ("grp", "seq"), axis=0, tiled=True)
+    upstream_all = lax.dynamic_slice_in_dim(up_four, group * group_slots, group_slots, 0)
     mixin = jnp.einsum(
-        "td,dcf->tcf", normed_low, mix_full, preferred_element_type=jnp.float32
-    ) + bias_full.astype(jnp.float32)
-    heads_in = mixin.reshape(slots_dev, 3, width // HEAD_DIM, HEAD_DIM)
-    sending = jnp.stack(
-        [
-            rotate(heads_in[:, 0], place_mine, 1.0),
-            rotate(heads_in[:, 1], place_mine, 1.0),
-            heads_in[:, 2],
-        ],
-        axis=1,
-    ).astype(jnp.bfloat16)
-    arrived = lax.all_to_all(
-        sending.reshape(slots_dev, 3, seq_count, local_width),
-        "seq",
-        split_axis=2,
-        concat_axis=0,
-        tiled=True,
-    )
-    arrived = arrived.reshape(group_slots, 3, local_heads, HEAD_DIM)
-    query, key, value = (arrived[:, 0], arrived[:, 1], arrived[:, 2])
+        "td,dcf->tcf", normed_all, mix_weight, preferred_element_type=jnp.float32
+    ) + mix_bias.astype(jnp.float32)
+    heads_in = mixin.reshape(group_slots, 3, local_heads, HEAD_DIM)
+    query = rotate(heads_in[:, 0], place_all, 1.0).astype(jnp.bfloat16)
+    key = rotate(heads_in[:, 1], place_all, 1.0).astype(jnp.bfloat16)
+    value = heads_in[:, 2].astype(jnp.bfloat16)
     mixed, log_totals = attend(query, key, value, label_all, block)
-    attended = lax.all_to_all(
-        mixed.reshape(group_slots, local_width).astype(jnp.bfloat16),
-        "seq",
-        split_axis=0,
-        concat_axis=1,
-        tiled=True,
-    )
-    resid = inputs + jnp.dot(attended, out_full, preferred_element_type=jnp.float32)
+    attended = mixed.reshape(group_slots, local_width).astype(jnp.bfloat16)
+
+    def out_product(part):
+        return jnp.dot(part, out_weight, preferred_element_type=jnp.float32)
+
+    resid = inputs + summed_rows(out_product, attended)
     normed_two, unit_two, scale_two = layer_norm(resid, norm_gains[1], norm_biases[1])
-    normed_two_all = gather_rows(normed_two.astype(jnp.bfloat16))
-    gate_up = jnp.einsum(
-        "td,dcf->tcf", normed_two_all, gate_up_weight, preferred_element_type=jnp.float32
-    )
-    hidden, gate, upper, sigma = silu_parts(gate_up)
-    hidden_low = hidden.astype(jnp.bfloat16)
+    normed_two_low = normed_two.astype(jnp.bfloat16)
+    normed_two_all = gather_rows(normed_two_low)
+    two_four = lax.all_gather(normed_two_low, ("grp", "seq"), axis=0, tiled=True)
+
+    def up_to_back(two, up):
+        gate_up = jnp.einsum("td,dcf->tcf", two, gate_up_weight, preferred_element_type=jnp.float32)
+        hidden, gate, upper, sigma = silu_parts(gate_up)
+        hidden_back = jnp.einsum("td,fd->tf", up, down_weight, preferred_element_type=jnp.float32)
+        return hidden.astype(jnp.bfloat16), gate_back(hidden_back, gate, upper, sigma)
+
+    hidden_low, gate_up_back = up_to_back(normed_two_all, upstream_all)
 
     def down_product(part):
         return jnp.dot(part, down_weight, preferred_element_type=jnp.float32)
 
     layer_out = resid + summed_rows(down_product, hidden_low)
-    upstream_all = gather_rows(upstream_low)
-    down_shard = jnp.einsum(
-        "tf,td->fd", hidden_low, upstream_all, preferred_element_type=jnp.float32
-    )
-    hidden_back = jnp.einsum(
-        "td,fd->tf", upstream_all, down_weight, preferred_element_type=jnp.float32
-    )
-    gate_up_back = gate_back(hidden_back, gate, upper, sigma)
-    gate_up_shard = jnp.einsum(
-        "td,tcf->dcf", normed_two_all, gate_up_back, preferred_element_type=jnp.float32
-    )
 
     def gate_up_product(part):
         return jnp.einsum("tcf,dcf->td", part, gate_up_weight, preferred_element_type=jnp.float32)
 
     normed_two_back = summed_rows(gate_up_product, gate_up_back)
+    hidden_four, back_four = up_to_back(two_four, up_four)
+    down_grad = jnp.einsum("tf,td->fd", hidden_four, up_four, preferred_element_type=jnp.float32)
+    gate_up_grad = jnp.einsum(
+        "td,tcf->dcf", two_four, back_four, preferred_element_type=jnp.float32
+    )
     resid_part, gain_two, bias_two = norm_back(normed_two_back, unit_two, scale_two, norm_gains[1])
     resid_back = upstream + resid_part
-    branch_low = resid_back.astype(jnp.bfloat16)
-    out_term = jnp.einsum("te,td->ed", attended, branch_low, preferred_element_type=jnp.float32)
+    branch_all = gather_rows(resid_back.astype(jnp.bfloat16))
+    out_term = jnp.einsum("te,td->ed", attended, branch_all, preferred_element_type=jnp.float32)
+    out_grad = lax.psum(out_term.astype(jnp.bfloat16), "grp").astype(jnp.float32)
     attended_back = jnp.einsum(
-        "td,ed->te", branch_low, out_full, preferred_element_type=jnp.float32
+        "td,ed->te", branch_all, out_weight, preferred_element_type=jnp.float32
     ).astype(jnp.bfloat16)
-    heads_back = lax.all_to_all(
-        attended_back, "seq", split_axis=1, concat_axis=0, tiled=True
-    ).reshape(group_slots, local_heads, HEAD_DIM)
+    heads_back = attended_back.reshape(group_slots, local_heads, HEAD_DIM)
     query_back, key_back, value_back = attend_back(
         query, key, value, label_all, log_totals, heads_back, block
     )
-    lowered = (
-        jnp.stack([query_back, key_back, value_back], axis=1)
-        .astype(jnp.bfloat16)
-        .reshape(group_slots, 3, 1, local_width)
-    )
-    returned = lax.all_to_all(lowered, "seq", split_axis=0, concat_axis=2, tiled=True).reshape(
-        slots_dev, 3, width // HEAD_DIM, HEAD_DIM
-    )
-    mixin_back = unrotate(returned, place_mine)
-    mix_term = jnp.einsum("td,tcf->dcf", normed_low, mixin_back, preferred_element_type=jnp.float32)
+    lowered = jnp.stack([query_back, key_back, value_back], axis=1).astype(jnp.bfloat16)
+    mixin_back = unrotate(lowered, place_all)
+    mix_term = jnp.einsum("td,tcf->dcf", normed_all, mixin_back, preferred_element_type=jnp.float32)
+    mix_grad = lax.psum(mix_term.astype(jnp.bfloat16), "grp").astype(jnp.float32)
     bias_term = jnp.sum(mixin_back, axis=0, dtype=jnp.float32)
-    normed_back = jnp.einsum(
-        "tcf,dcf->td", mixin_back, mix_full, preferred_element_type=jnp.float32
-    )
-    mix_shard, bias_shard, out_shard = (
-        lax.psum_scatter(
-            mix_term.astype(jnp.bfloat16), "seq", scatter_dimension=2, tiled=True
-        ).astype(jnp.float32),
-        lax.psum_scatter(
-            bias_term.astype(jnp.bfloat16), "seq", scatter_dimension=1, tiled=True
-        ).astype(jnp.float32),
-        lax.psum_scatter(
-            out_term.astype(jnp.bfloat16), "seq", scatter_dimension=0, tiled=True
-        ).astype(jnp.float32),
-    )
+    mix_bias_grad = lax.psum(bias_term, "grp")
+
+    def mix_product(part):
+        return jnp.einsum("tcf,dcf->td", part, mix_weight, preferred_element_type=jnp.float32)
+
+    normed_back = summed_rows(mix_product, mixin_back)
     tokens_part, gain_one, bias_one = norm_back(normed_back, unit_one, scale_one, norm_gains[0])
     tokens_grad = (resid_back + tokens_part).astype(jnp.bfloat16)
-    mix_grad, mix_bias_grad, out_grad, gate_up_grad, down_grad = (
-        lax.psum(mix_shard.astype(jnp.bfloat16), "grp").astype(jnp.float32),
-        lax.psum(bias_shard.astype(jnp.bfloat16), "grp").astype(jnp.float32),
-        lax.psum(out_shard.astype(jnp.bfloat16), "grp").astype(jnp.float32),
-        lax.psum(gate_up_shard.astype(jnp.bfloat16), "grp").astype(jnp.float32),
-        lax.psum(down_shard.astype(jnp.bfloat16), "grp").astype(jnp.float32),
-    )
     gains_grad, biases_grad = lax.psum(
         (jnp.stack([gain_one, gain_two]), jnp.stack([bias_one, bias_two])), ("grp", "seq")
     )
@@ -307,6 +268,829 @@
         mix_bias_grad,
         out_grad,
         gate_up_grad,
+        down_grad,
+    )
+
+
+MESH_ID = pl.DeviceIdType.MESH
+N_RS = 10
+N_AG = 13
+
+
+class Ring:
+    def __init__(self):
+        self.group = lax.axis_index("grp")
+        self.me = lax.axis_index("seq")
+        core = self.me % 2
+        x = (self.me // 2) % 2
+        y = self.me // 4
+        self.flip = 1 - 2 * core
+        self.twin = self.me + self.flip
+        self.xn = self.me + 2 - 4 * x
+        self.yn = self.me + 4 - 8 * y
+        self.dn = self.xn + 4 - 8 * y
+
+    def dev(self, seq):
+        return (self.group, seq)
+
+    def barrier(self, extra=()):
+        sem = pltpu.get_barrier_semaphore()
+        peers = [self.dev(self.twin), self.dev(self.xn), self.dev(self.yn)] + list(extra)
+        for peer in peers:
+            pl.semaphore_signal(sem, inc=1, device_id=peer, device_id_type=MESH_ID)
+        pl.semaphore_wait(sem, len(peers))
+
+    def copy(self, src, dst, send, recv, kind, seq):
+        return pltpu.make_async_remote_copy(
+            src_ref=src,
+            dst_ref=dst,
+            send_sem=send.at[kind],
+            recv_sem=recv.at[kind],
+            device_id=self.dev(seq),
+            device_id_type=MESH_ID,
+        )
+
+
+def gather_steps(ring, own, out, send, recv, local):
+    rows = own.shape[0]
+    half = rows // 2
+
+    def at(block, part=None):
+        if part is None:
+            return out.at[pl.ds(pl.multiple_of(block * rows, rows), rows), :]
+        return out.at[pl.ds(pl.multiple_of(block * rows + part * half, half), half), :]
+
+    def go(src, dst, kind, seq):
+        copy = ring.copy(src, dst, send, recv, kind, seq)
+        copy.start()
+        return copy
+
+    keep = pltpu.make_async_copy(own, at(ring.me), local)
+    keep.start()
+    lo, hi = own.at[pl.ds(0, half), :], own.at[pl.ds(half, half), :]
+    x0 = go(lo, at(ring.me, 0), 0, ring.xn)
+    y1 = go(hi, at(ring.me, 1), 1, ring.yn)
+    x1 = go(hi, at(ring.me, 1), 2, ring.xn)
+    y0 = go(lo, at(ring.me, 0), 3, ring.yn)
+    t0 = go(own, at(ring.me), 4, ring.twin)
+    x0.wait_recv()
+    f0 = go(at(ring.xn, 0), at(ring.xn, 0), 5, ring.yn)
+    t1 = go(at(ring.xn, 0), at(ring.xn, 0), 6, ring.twin)
+    y1.wait_recv()
+    f1 = go(at(ring.yn, 1), at(ring.yn, 1), 7, ring.xn)
+    t2 = go(at(ring.yn, 1), at(ring.yn, 1), 8, ring.twin)
+    x1.wait_recv()
+    t3 = go(at(ring.xn, 1), at(ring.xn, 1), 9, ring.twin)
+    y0.wait_recv()
+    t4 = go(at(ring.yn, 0), at(ring.yn, 0), 10, ring.twin)
+    f0.wait_recv()
+    t5 = go(at(ring.dn, 0), at(ring.dn, 0), 11, ring.twin)
+    f1.wait_recv()
+    t6 = go(at(ring.dn, 1), at(ring.dn, 1), 12, ring.twin)
+    keep.wait()
+    for copy in (t0, t1, t2, t3, t4, t5, t6):
+        copy.wait_recv()
+    for copy in (x0, y1, x1, y0, f0, f1, t0, t1, t2, t3, t4, t5, t6):
+        copy.wait_send()
+
+
+def scatter_steps(ring, part, total, own, pair, rx, ry, fx, fy, stage, send, recv, local):
+    rows, width = total.shape
+    half = width // 2
+    wide = jnp.float32
+    order = [ring.dn, ring.xn, ring.yn, ring.me]
+
+    def block(index):
+        return part.at[pl.ds(pl.multiple_of(index * rows, rows), rows), :]
+
+    pairs, keeps = [], []
+    for slot, index in enumerate(order):
+        copy = ring.copy(block(index + ring.flip), pair.at[slot], send, recv, slot, ring.twin)
+        copy.start()
+        pairs.append(copy)
+        keep = pltpu.make_async_copy(block(index), own.at[slot], local.at[slot])
+        keep.start()
+        keeps.append(keep)
+
+    def go(src, dst, kind, seq):
+        copy = ring.copy(src, dst, send, recv, kind, seq)
+        copy.start()
+        return copy
+
+    def added(slot):
+        keeps[slot].wait()
+        pairs[slot].wait_recv()
+        return own[slot].astype(wide) + pair[slot].astype(wide)
+
+    lo, hi = pl.ds(0, half), pl.ds(half, half)
+    own[0] = added(0).astype(own.dtype)
+    x0 = go(own.at[0, :, lo], rx.at[0], 4, ring.xn)
+    y0 = go(own.at[0, :, hi], ry.at[0], 5, ring.yn)
+    own[1] = added(1).astype(own.dtype)
+    x1 = go(own.at[1, :, lo], rx.at[1], 6, ring.xn)
+    own[2] = added(2).astype(own.dtype)
+    y1 = go(own.at[2, :, hi], ry.at[1], 7, ring.yn)
+    total[...] = added(3)
+    x0.wait_recv()
+    stage[0] = (own[2, :, lo].astype(wide) + rx[0].astype(wide)).astype(own.dtype)
+    gy = go(stage.at[0], fy, 8, ring.yn)
+    y0.wait_recv()
+    stage[1] = (own[1, :, hi].astype(wide) + ry[0].astype(wide)).astype(own.dtype)
+    gx = go(stage.at[1], fx, 9, ring.xn)
+    x1.wait_recv()
+    total[:, lo] += rx[1].astype(wide)
+    y1.wait_recv()
+    total[:, hi] += ry[1].astype(wide)
+    gy.wait_recv()
+    total[:, lo] += fy[...].astype(wide)
+    gx.wait_recv()
+    total[:, hi] += fx[...].astype(wide)
+    for copy in pairs + [x0, y0, x1, y1, gy, gx]:
+        copy.wait_send()
+
+
+def scatter_scratch(rows, width):
+    low = jnp.bfloat16
+    half = width // 2
+    return [
+        pltpu.VMEM((rows, width), jnp.float32),
+        pltpu.VMEM((4, rows, width), low),
+        pltpu.VMEM((4, rows, width), low),
+        pltpu.VMEM((2, rows, half), low),
+        pltpu.VMEM((2, rows, half), low),
+        pltpu.VMEM((rows, half), low),
+        pltpu.VMEM((rows, half), low),
+        pltpu.VMEM((2, rows, half), low),
+        pltpu.SemaphoreType.DMA((N_RS,)),
+        pltpu.SemaphoreType.DMA((N_RS,)),
+        pltpu.SemaphoreType.DMA((4,)),
+    ]
+
+
+def gather_scratch(rows, width):
+    return [
+        pltpu.VMEM((rows, width), jnp.bfloat16),
+        pltpu.SemaphoreType.DMA((N_AG,)),
+        pltpu.SemaphoreType.DMA((N_AG,)),
+        pltpu.SemaphoreType.DMA,
+    ]
+
+
+def unit_of(values):
+    centered = values - jnp.mean(values, axis=-1, keepdims=True)
+    scale = lax.rsqrt(jnp.mean(centered * centered, axis=-1, keepdims=True) + EPS)
+    return centered * scale, scale
+
+
+def back_of(incoming, unit, scale, gain):
+    along = incoming * gain
+    inner = jnp.mean(along, axis=-1, keepdims=True)
+    cross = jnp.mean(along * unit, axis=-1, keepdims=True)
+    return scale * (along - inner - unit * cross)
+
+
+def first_kernel(tokens, gains, biases, normed_all, own, send, recv, local):
+    ring = Ring()
+    unit, _ = unit_of(tokens[...].astype(jnp.float32))
+    own[...] = (unit * gains[0:1] + biases[0:1]).astype(own.dtype)
+    ring.barrier()
+    gather_steps(ring, own, normed_all, send, recv, local)
+
+
+def second_kernel(part, tokens, gains, biases, resid, two_all, *scratch):
+    rs, ag = scratch[:11], scratch[11:]
+    ring = Ring()
+    ring.barrier()
+    scatter_steps(ring, part, *rs)
+    total, own = rs[0], ag[0]
+    resid[...] = total[...] + tokens[...].astype(jnp.float32)
+    unit, _ = unit_of(resid[...])
+    own[...] = (unit * gains[1:2] + biases[1:2]).astype(own.dtype)
+    gather_steps(ring, own, two_all, *ag[1:])
+
+
+def third_kernel(part, resid, upstream, gains, resid_back, branch_all, sums, *scratch):
+    rs, ag = scratch[:11], scratch[11:]
+    ring = Ring()
+    ring.barrier()
+    scatter_steps(ring, part, *rs)
+    total, own = rs[0], ag[0]
+    unit, scale = unit_of(resid[...])
+    incoming = total[...]
+    resid_back[...] = upstream[...].astype(jnp.float32) + back_of(incoming, unit, scale, gains[1:2])
+    own[...] = resid_back[...].astype(own.dtype)
+    sums[0:1] = jnp.sum(incoming * unit, axis=0, keepdims=True)
+    sums[1:2] = jnp.sum(incoming, axis=0, keepdims=True)
+    gather_steps(ring, own, branch_all, *ag[1:])
+
+
+def fourth_kernel(part, tokens, resid_back, gains, sums, tokens_grad, four, *scratch):
+    rs, (inbox, mail, send, recv) = scratch[:11], scratch[11:]
+    ring = Ring()
+    groups = lax.axis_size("grp")
+    others = [(lax.rem(ring.group + k, groups), ring.me) for k in range(1, groups)]
+    ring.barrier(others)
+    scatter_steps(ring, part, *rs)
+    unit, scale = unit_of(tokens[...].astype(jnp.float32))
+    incoming = rs[0][...]
+    tokens_grad[...] = (resid_back[...] + back_of(incoming, unit, scale, gains[0:1])).astype(
+        tokens_grad.dtype
+    )
+    four[0:1] = jnp.sum(incoming * unit, axis=0, keepdims=True)
+    four[1:2] = sums[0:1]
+    four[2:3] = jnp.sum(incoming, axis=0, keepdims=True)
+    four[3:4] = sums[1:2]
+    for stage, peer in enumerate((ring.twin, ring.xn, ring.yn)):
+        mail[stage] = four[...]
+        copy = ring.copy(mail.at[stage], inbox.at[stage], send, recv, stage, peer)
+        copy.start()
+        copy.wait_recv()
+        four[...] += inbox[stage]
+        copy.wait_send()
+    mail[3] = four[...]
+    copies = []
+    for k, peer in enumerate(others):
+        copy = pltpu.make_async_remote_copy(
+            src_ref=mail.at[3],
+            dst_ref=inbox.at[3 + k],
+            send_sem=send.at[3 + k],
+            recv_sem=recv.at[3 + k],
+            device_id=peer,
+            device_id_type=MESH_ID,
+        )
+        copy.start()
+        copies.append(copy)
+    for copy in copies:
+        copy.wait_recv()
+    total = jnp.zeros(four.shape, jnp.float32)
+    for group in range(groups):
+        term = mail[3]
+        for k in range(1, groups):
+            source = lax.rem(ring.group + groups - k, groups)
+            term = jnp.where(source == group, inbox[2 + k], term)
+        total = total + term
+    four[...] = total
+    for copy in copies:
+        copy.wait_send()
+
+
+VM = pl.BlockSpec(memory_space=pltpu.VMEM)
+ANY = pl.BlockSpec(memory_space=pl.ANY)
+
+
+def call(kernel, number, ins, outs, scratch, cost=20_000_000):
+    return pl.pallas_call(
+        kernel,
+        out_shape=tuple(jax.ShapeDtypeStruct(*shape) for shape, _ in outs),
+        in_specs=[spec for _, spec in ins],
+        out_specs=tuple(spec for _, spec in outs),
+        scratch_shapes=scratch,
+        compiler_params=pltpu.CompilerParams(
+            collective_id=number, has_side_effects=True, vmem_limit_bytes=40 << 20
+        ),
+        cost_estimate=pl.CostEstimate(flops=0, bytes_accessed=cost, transcendentals=0),
+    )(*[value for value, _ in ins])
+
+
+def first(tokens, gains, biases, count):
+    rows, width = tokens.shape
+    low = jnp.bfloat16
+    return call(
+        first_kernel,
+        1,
+        [(tokens, VM), (gains, VM), (biases, VM)],
+        [(((rows * count, width), low), ANY)],
+        gather_scratch(rows, width),
+    )[0]
+
+
+def second(part, tokens, gains, biases, count):
+    rows, width = tokens.shape
+    return call(
+        second_kernel,
+        2,
+        [(part, ANY), (tokens, VM), (gains, VM), (biases, VM)],
+        [(((rows, width), jnp.float32), VM), (((rows * count, width), jnp.bfloat16), ANY)],
+        scatter_scratch(rows, width) + gather_scratch(rows, width),
+    )
+
+
+def third(part, resid, upstream, gains, count):
+    rows, width = resid.shape
+    return call(
+        third_kernel,
+        3,
+        [(part, ANY), (resid, VM), (upstream, VM), (gains, VM)],
+        [
+            (((rows, width), jnp.float32), VM),
+            (((rows * count, width), jnp.bfloat16), ANY),
+            (((2, width), jnp.float32), VM),
+        ],
+        scatter_scratch(rows, width) + gather_scratch(rows, width),
+    )
+
+
+def fourth(part, tokens, resid_back, gains, sums):
+    rows, width = tokens.shape
+    groups = lax.axis_size("grp")
+    return call(
+        fourth_kernel,
+        4,
+        [(part, ANY), (tokens, VM), (resid_back, VM), (gains, VM), (sums, VM)],
+        [(((rows, width), jnp.bfloat16), VM), (((4, width), jnp.float32), VM)],
+        scatter_scratch(rows, width)
+        + [
+            pltpu.VMEM((2 + groups, 4, width), jnp.float32),
+            pltpu.VMEM((4, 4, width), jnp.float32),
+            pltpu.SemaphoreType.DMA((2 + groups,)),
+            pltpu.SemaphoreType.DMA((2 + groups,)),
+        ],
+    )
+
+
+TILE = 256
+WIDE = jnp.float32
+LOW = jnp.bfloat16
+NT = (((1,), (1,)), ((), ()))
+TN = (((0,), (0,)), ((), ()))
+
+
+def mm(a, b, dims=(((1,), (0,)), ((), ()))):
+    return lax.dot_general(a, b, dims, preferred_element_type=WIDE)
+
+
+def head_lanes(shape, head):
+    return lax.broadcasted_iota(jnp.int32, shape, 1) // HEAD_DIM == head
+
+
+def turn(u, tables, rows, sign):
+    cosine, below, above = (
+        jnp.concatenate([tables[i, rows, :]] * (u.shape[1] // 128), axis=1) for i in range(3)
+    )
+    side = pltpu.roll(u, 8, 1) * below + pltpu.roll(u, u.shape[1] - 8, 1) * above
+    return u * cosine + side if sign > 0 else u * cosine - side
+
+
+def load(pairs, sems):
+    copies = []
+    for i, (src, dst) in enumerate(pairs):
+        copy = pltpu.make_async_copy(src, dst, sems.at[i])
+        copy.start()
+        copies.append(copy)
+    return copies
+
+
+def attend_kernel(
+    normed_all, weight, out_weight, bias, tables, lab_col, lab_row,
+    query, key, value, attended, lse, part,
+    normed, w, mask, stats, stage, sems, outs,
+):
+    total, width = query.shape
+    tiles = total // TILE
+    loads = load(
+        [(normed_all.at[pl.ds(i * TILE, TILE), :], normed.at[pl.ds(i * TILE, TILE), :]) for i in range(tiles)]
+        + [(weight, w)],
+        sems,
+    )
+    loads[-1].wait()
+    for i in range(tiles):
+        rows = pl.ds(i * TILE, TILE)
+        loads[i].wait()
+        x = normed[rows, :]
+        u = mm(x, w[0]) + bias[0:1]
+        query[rows, :] = (turn(u, tables, rows, 1).astype(LOW).astype(WIDE) * (1.0 / 8)).astype(LOW)
+        u = mm(x, w[1]) + bias[1:2]
+        key[rows, :] = turn(u, tables, rows, 1).astype(LOW)
+        value[rows, :] = (mm(x, w[2]) + bias[2:3]).astype(LOW)
+    copies = []
+    for i in range(tiles):
+        rows = pl.ds(i * TILE, TILE)
+        span = (i + 1) * TILE
+        q_at = i * TILE + lax.broadcasted_iota(jnp.int32, (TILE, span), 0)
+        k_at = lax.broadcasted_iota(jnp.int32, (TILE, span), 1)
+        allowed = (lab_col[rows, :] == lab_row[:, :span]) & (q_at >= k_at)
+        mask[:, :span] = jnp.where(allowed, 0.0, NEG)
+        q = query[rows, :]
+
+        def one_head(head, carry):
+            mixed, logs = carry
+            mine = head_lanes(q.shape, head)
+            s = mm(jnp.where(mine, q, jnp.zeros_like(q)), key[:span, :], NT) + mask[:, :span]
+            top = jnp.max(s, axis=1, keepdims=True)
+            p = jnp.exp(s - top)
+            norm = jnp.sum(p, axis=1, keepdims=True)
+            o = mm(p.astype(LOW), value[:span, :]) / norm
+            mixed = jnp.where(mine, o, mixed)
+            lane = lax.broadcasted_iota(jnp.int32, logs.shape, 1)
+            logs = jnp.where(lane == head, top + jnp.log(norm), logs)
+            return mixed, logs
+
+        mixed, logs = lax.fori_loop(
+            0, width // HEAD_DIM, one_head,
+            (jnp.zeros((TILE, width), WIDE), jnp.zeros((TILE, 128), WIDE)),
+        )
+        low = mixed.astype(LOW)
+        attended[rows, :] = low
+        stats[rows, :] = logs
+        stage[i] = mm(low, out_weight[...]).astype(LOW)
+        copy = pltpu.make_async_copy(stage.at[i], part.at[rows, :], outs.at[i])
+        copy.start()
+        copies.append(copy)
+    lse[...] = jnp.transpose(stats[...])[:8, :]
+    for copy in copies:
+        copy.wait()
+
+
+def attend_heads(normed_all, weight, out_weight, bias, tables, lab_col, lab_row):
+    total, width = normed_all.shape
+    local = out_weight.shape[0]
+    tiles = total // TILE
+    slab = jax.ShapeDtypeStruct((total, local), LOW)
+    return pl.pallas_call(
+        attend_kernel,
+        out_shape=(
+            slab, slab, slab, slab,
+            jax.ShapeDtypeStruct((8, total), WIDE),
+            jax.ShapeDtypeStruct((total, width), LOW),
+        ),
+        in_specs=[ANY, ANY, VM, VM, VM, VM, VM],
+        out_specs=(VM, VM, VM, VM, VM, ANY),
+        scratch_shapes=[
+            pltpu.VMEM((total, width), LOW),
+            pltpu.VMEM((3, width, local), LOW),
+            pltpu.VMEM((TILE, total), WIDE),
+            pltpu.VMEM((total, 128), WIDE),
+            pltpu.VMEM((tiles, TILE, width), LOW),
+            pltpu.SemaphoreType.DMA((tiles + 1,)),
+            pltpu.SemaphoreType.DMA((tiles,)),
+        ],
+        compiler_params=pltpu.CompilerParams(vmem_limit_bytes=48 << 20),
+        cost_estimate=pl.CostEstimate(flops=7 << 30, bytes_accessed=16 << 20, transcendentals=4 << 20),
+    )(normed_all, weight, out_weight, bias, tables, lab_col, lab_row)
+
+
+def attend_back_kernel(
+    branch_all, normed_all, weight, out_weight, tables, lab_col, lab_row,
+    query, key, value, attended, lse,
+    part, mix_term, out_term, bias_term,
+    branch, normed, w, mask, inner, heads_back, query_back, key_back, value_back, mixin, stage, mixes,
+    sems, outs,
+):
+    total, width = query.shape
+    tiles = total // TILE
+    heads = width // HEAD_DIM
+    loads = load(
+        [(branch_all.at[pl.ds(i * TILE, TILE), :], branch.at[pl.ds(i * TILE, TILE), :]) for i in range(tiles)]
+        + [(normed_all, normed), (weight, w)],
+        sems,
+    )
+    head_of = lax.broadcasted_iota(jnp.int32, (8, width), 1) // HEAD_DIM
+    pick = (head_of == lax.broadcasted_iota(jnp.int32, (8, width), 0)).astype(LOW)
+    for i in range(tiles):
+        rows = pl.ds(i * TILE, TILE)
+        loads[i].wait()
+        low = mm(branch[rows, :], out_weight[...], NT).astype(LOW)
+        heads_back[rows, :] = low
+        prod = low.astype(WIDE) * attended[rows, :].astype(WIDE)
+        high = prod.astype(LOW)
+        rest = (prod - high.astype(WIDE)).astype(LOW)
+        inner[:, rows] = mm(pick, high, NT) + mm(pick, rest, NT)
+    out_term[...] = mm(attended[...], branch[...], TN).astype(LOW)
+    key_back[...] = jnp.zeros_like(key_back)
+    value_back[...] = jnp.zeros_like(value_back)
+    for i in range(tiles):
+        rows = pl.ds(i * TILE, TILE)
+        span = (i + 1) * TILE
+        k_at = lax.broadcasted_iota(jnp.int32, (span, TILE), 0)
+        q_at = i * TILE + lax.broadcasted_iota(jnp.int32, (span, TILE), 1)
+        allowed = (lab_col[:span, :] == lab_row[:, rows]) & (q_at >= k_at)
+        mask[:span, :] = jnp.where(allowed, 0.0, NEG)
+        q = query[rows, :]
+        d_out = heads_back[rows, :]
+
+        def one_head(head, q_back):
+            mine = head_lanes(q.shape, head)
+            q_h = jnp.where(mine, q, jnp.zeros_like(q))
+            d_h = jnp.where(mine, d_out, jnp.zeros_like(q))
+            k = key[:span, :]
+            k_h = jnp.where(head_lanes(k.shape, head), k, jnp.zeros_like(k))
+            p = jnp.exp(mm(k, q_h, NT) + mask[:span, :] - lse[pl.ds(head, 1), rows])
+            d_p = mm(value[:span, :], d_h, NT)
+            d_s = (p * (d_p - inner[pl.ds(head, 1), rows])).astype(LOW)
+            value_back[:span, :] += mm(p.astype(LOW), d_h)
+            key_back[:span, :] += mm(d_s, q_h)
+            return q_back + mm(d_s, k_h, TN)
+
+        query_back[rows, :] = lax.fori_loop(0, heads, one_head, jnp.zeros((TILE, width), WIDE))
+    loads[-1].wait()
+    loads[-2].wait()
+    copies = []
+    sums = [jnp.zeros((1, width), WIDE)] * 3
+    for i in range(tiles):
+        rows = pl.ds(i * TILE, TILE)
+        q_b = (query_back[rows, :] * (1.0 / 8)).astype(LOW).astype(WIDE)
+        k_b = key_back[rows, :].astype(LOW).astype(WIDE)
+        trio = [
+            turn(q_b, tables, rows, -1).astype(LOW),
+            turn(k_b, tables, rows, -1).astype(LOW),
+            value_back[rows, :].astype(LOW),
+        ]
+        product = jnp.zeros((TILE, normed.shape[1]), WIDE)
+        for c, item in enumerate(trio):
+            mixin[c, rows, :] = item
+            sums[c] = sums[c] + jnp.sum(item.astype(WIDE), axis=0, keepdims=True)
+            product = product + mm(item, w[c], NT)
+        stage[i] = product.astype(LOW)
+        copy = pltpu.make_async_copy(stage.at[i], part.at[rows, :], outs.at[i])
+        copy.start()
+        copies.append(copy)
+    for c in range(3):
+        bias_term[c : c + 1, :] = sums[c]
+        mixes[c] = mm(normed[...], mixin[c], TN).astype(LOW)
+        copy = pltpu.make_async_copy(mixes.at[c], mix_term.at[c], outs.at[tiles + c])
+        copy.start()
+        copies.append(copy)
+    for copy in copies:
+        copy.wait()
+
+
+def attend_heads_back(branch_all, normed_all, weight, out_weight, tables, lab_col, lab_row, saved):
+    total, width = normed_all.shape
+    local = out_weight.shape[0]
+    tiles = total // TILE
+    return pl.pallas_call(
+        attend_back_kernel,
+        out_shape=(
+            jax.ShapeDtypeStruct((total, width), LOW),
+            jax.ShapeDtypeStruct((3, width, local), LOW),
+            jax.ShapeDtypeStruct((local, width), LOW),
+            jax.ShapeDtypeStruct((3, local), WIDE),
+        ),
+        in_specs=[ANY, ANY, ANY] + [VM] * 9,
+        out_specs=(ANY, ANY, VM, VM),
+        scratch_shapes=[
+            pltpu.VMEM((total, width), LOW),
+            pltpu.VMEM((total, width), LOW),
+            pltpu.VMEM((3, width, local), LOW),
+            pltpu.VMEM((total, TILE), WIDE),
+            pltpu.VMEM((8, total), WIDE),
+            pltpu.VMEM((total, local), LOW),
+            pltpu.VMEM((total, local), WIDE),
+            pltpu.VMEM((total, local), WIDE),
+            pltpu.VMEM((total, local), WIDE),
+            pltpu.VMEM((3, total, local), LOW),
+            pltpu.VMEM((tiles, TILE, width), LOW),
+            pltpu.VMEM((3, width, local), LOW),
+            pltpu.SemaphoreType.DMA((tiles + 2,)),
+            pltpu.SemaphoreType.DMA((tiles + 3,)),
+        ],
+        compiler_params=pltpu.CompilerParams(vmem_limit_bytes=60 << 20),
+        cost_estimate=pl.CostEstimate(flops=16 << 30, bytes_accessed=30 << 20, transcendentals=4 << 20),
+    )(branch_all, normed_all, weight, out_weight, tables, lab_col, lab_row, *saved)
+
+
+def units(gate, upper, hidden_back):
+    sigma = jax.nn.sigmoid(gate)
+    silu = gate * sigma
+    return (
+        (silu * upper).astype(LOW),
+        (hidden_back * upper * sigma * (1.0 + gate * (1.0 - sigma))).astype(LOW),
+        (hidden_back * silu).astype(LOW),
+    )
+
+
+def forward_units(two, up, wide, down):
+    return units(mm(wide[0], two, NT), mm(wide[1], two, NT), mm(down[...], up, NT))
+
+
+def feed_kernel(two_all, up_all, wide_hbm, down_hbm, back_part, down_part, saved,
+                two, up, wide, down, kept, stage, sems, outs):
+    total = two_all.shape[0]
+    tiles = total // TILE
+    pairs = [(wide_hbm, wide), (down_hbm, down)]
+    for i in range(tiles):
+        rows = pl.ds(i * TILE, TILE)
+        pairs += [(two_all.at[rows, :], two.at[rows, :]), (up_all.at[rows, :], up.at[rows, :])]
+    loads = load(pairs, sems)
+    loads[0].wait()
+    loads[1].wait()
+    copies = []
+    for i in range(tiles):
+        rows = pl.ds(i * TILE, TILE)
+        loads[2 + 2 * i].wait()
+        loads[3 + 2 * i].wait()
+        trio = forward_units(two[rows, :], up[rows, :], wide, down)
+        for c in range(3):
+            kept[c, :, rows] = trio[c]
+        stage[0, rows, :] = (mm(trio[1], wide[0], TN) + mm(trio[2], wide[1], TN)).astype(LOW)
+        copy = pltpu.make_async_copy(stage.at[0, rows, :], back_part.at[rows, :], outs.at[2 * i])
+        copy.start()
+        copies.append(copy)
+        stage[1, rows, :] = mm(trio[0], down[...], TN).astype(LOW)
+        copy = pltpu.make_async_copy(stage.at[1, rows, :], down_part.at[rows, :], outs.at[2 * i + 1])
+        copy.start()
+        copies.append(copy)
+    copy = pltpu.make_async_copy(kept, saved, outs.at[2 * tiles])
+    copy.start()
+    copy.wait()
+    for copy in copies:
+        copy.wait()
+
+
+def feed(two_all, up_all, wide, down):
+    total, width = two_all.shape
+    units_local = down.shape[0]
+    tiles = total // TILE
+    part = jax.ShapeDtypeStruct((total, width), LOW)
+    return pl.pallas_call(
+        feed_kernel,
+        out_shape=(part, part, jax.ShapeDtypeStruct((3, units_local, total), LOW)),
+        in_specs=[ANY] * 4,
+        out_specs=(ANY, ANY, ANY),
+        scratch_shapes=[
+            pltpu.VMEM((total, width), LOW),
+            pltpu.VMEM((total, width), LOW),
+            pltpu.VMEM((2, units_local, width), LOW),
+            pltpu.VMEM((units_local, width), LOW),
+            pltpu.VMEM((3, units_local, total), LOW),
+            pltpu.VMEM((2, total, width), LOW),
+            pltpu.SemaphoreType.DMA((2 + 2 * tiles,)),
+            pltpu.SemaphoreType.DMA((1 + 2 * tiles,)),
+        ],
+        compiler_params=pltpu.CompilerParams(vmem_limit_bytes=56 << 20),
+        cost_estimate=pl.CostEstimate(flops=18 << 30, bytes_accessed=40 << 20, transcendentals=1 << 20),
+    )(two_all, up_all, wide, down)
+
+
+BIG = 512
+
+
+def grads_kernel(two_all, up_all, saved, two_four, up_four, wide_hbm, down_hbm, wide_grad, down_grad,
+                 two, up, wide, down, kept, acc, sems, outs):
+    total = two_all.shape[0]
+    groups = two_four.shape[0] // total
+    group = lax.axis_index("grp")
+    per = total // BIG
+    weights = load([(wide_hbm, wide), (down_hbm, down)], sems.at[4])
+    keep = pltpu.make_async_copy(saved, kept, sems.at[4, 2])
+    keep.start()
+
+    def fetch(source_two, source_up, start, slot):
+        return [
+            pltpu.make_async_copy(source_two.at[pl.ds(pl.multiple_of(start, BIG), BIG), :], two.at[slot], sems.at[slot, 0]),
+            pltpu.make_async_copy(source_up.at[pl.ds(pl.multiple_of(start, BIG), BIG), :], up.at[slot], sems.at[slot, 1]),
+        ]
+
+    def other_start(step):
+        index = lax.rem(group + 1 + step // per, groups)
+        return index * total + lax.rem(step, per) * BIG
+
+    for copy in fetch(two_all, up_all, 0, 0):
+        copy.start()
+    keep.wait()
+    acc[...] = jnp.zeros_like(acc)
+
+    def add(slot, trio):
+        acc[2] += mm(trio[0], up[slot])
+        acc[0] += mm(trio[1], two[slot])
+        acc[1] += mm(trio[2], two[slot])
+
+    for i in range(per):
+        slot = i % 2
+        if i + 1 < per:
+            nxt = fetch(two_all, up_all, (i + 1) * BIG, 1 - slot)
+        else:
+            nxt = fetch(two_four, up_four, other_start(0), 1 - slot)
+        for copy in nxt:
+            copy.start()
+        for copy in fetch(two_all, up_all, 0, slot):
+            copy.wait()
+        add(slot, [kept[c, :, pl.ds(i * BIG, BIG)] for c in range(3)])
+    for copy in weights:
+        copy.wait()
+    steps = (groups - 1) * per
+
+    def body(step, carry):
+        slot = lax.rem(step + per, 2)
+        for copy in fetch(two_four, up_four, 0, slot):
+            copy.wait()
+
+        @pl.when(step + 1 < steps)
+        def _():
+            for copy in fetch(two_four, up_four, other_start(step + 1), 1 - slot):
+                copy.start()
+
+        add(slot, forward_units(two[slot], up[slot], wide, down))
+        return carry
+
+    lax.fori_loop(0, steps, body, 0)
+    copies = load([(acc.at[pl.ds(0, 2)], wide_grad), (acc.at[2], down_grad)], outs)
+    for copy in copies:
+        copy.wait()
+
+
+def grads(two_all, up_all, saved, two_four, up_four, wide, down):
+    total, width = two_all.shape
+    local = down.shape[0]
+    return pl.pallas_call(
+        grads_kernel,
+        out_shape=(jax.ShapeDtypeStruct((2, local, width), WIDE), jax.ShapeDtypeStruct((local, width), WIDE)),
+        in_specs=[ANY] * 7,
+        out_specs=(ANY, ANY),
+        scratch_shapes=[
+            pltpu.VMEM((2, BIG, width), LOW),
+            pltpu.VMEM((2, BIG, width), LOW),
+            pltpu.VMEM((2, local, width), LOW),
+            pltpu.VMEM((local, width), LOW),
+            pltpu.VMEM((3, local, total), LOW),
+            pltpu.VMEM((3, local, width), WIDE),
+            pltpu.SemaphoreType.DMA((5, 3)),
+            pltpu.SemaphoreType.DMA((2,)),
+        ],
+        compiler_params=pltpu.CompilerParams(vmem_limit_bytes=60 << 20),
+        cost_estimate=pl.CostEstimate(flops=60 << 30, bytes_accessed=60 << 20, transcendentals=4 << 20),
+    )(two_all, up_all, saved, two_four, up_four, wide, down)
+
+
+RING = 8
+
+
+def rope_tables(place):
+    half = ROT // 2
+    freq = BASE ** (-jnp.arange(half, dtype=jnp.float32) / half)
+    angle = place.astype(jnp.float32)[:, None] * freq[None, :]
+    cosine, sine = lax.optimization_barrier((jnp.cos(angle), jnp.sin(angle)))
+    lane = jnp.arange(128) % HEAD_DIM
+    cosine = jnp.where(lane < ROT, jnp.tile(cosine, (1, 128 // half)), 1.0)
+    sine = jnp.tile(sine, (1, 128 // half))
+    return jnp.stack(
+        [
+            cosine,
+            jnp.where((lane >= half) & (lane < ROT), sine, 0.0),
+            jnp.where(lane < half, -sine, 0.0),
+        ]
+    )
+
+
+def on_device(
+    tokens,
+    norm_gains,
+    norm_biases,
+    mix_weight,
+    mix_bias,
+    out_weight,
+    gate_up_weight,
+    down_weight,
+    row_lengths,
+    row_group,
+    cotangent,
+):
+    count = lax.axis_size("seq")
+    shard = lax.axis_index("seq")
+    group = lax.axis_index("grp")
+    slots_dev = tokens.shape[0]
+    group_slots = slots_dev * count
+    label_all, place_all = slot_rows(
+        row_lengths, row_group, group, jnp.arange(group_slots, dtype=jnp.int32)
+    )
+    label_mine = lax.dynamic_slice_in_dim(label_all, shard * slots_dev, slots_dev, 0)
+    upstream = jnp.where(label_mine[:, None] >= 0, cotangent, jnp.zeros_like(cotangent))
+    lab_col, lab_row = label_all[:, None], label_all[None, :]
+    tables = rope_tables(place_all)
+    mix_t = jnp.transpose(mix_weight, (1, 0, 2))
+    wide_t = jnp.transpose(gate_up_weight, (1, 2, 0))
+
+    normed_all = first(tokens, norm_gains, norm_biases, count)
+    up_four = lax.all_gather(upstream, ("grp", "seq"), axis=0, tiled=True)
+    query, key, value, attended, lse, part = attend_heads(
+        normed_all, mix_t, out_weight, mix_bias.astype(jnp.float32), tables, lab_col, lab_row
+    )
+    resid, two_all = second(part, tokens, norm_gains, norm_biases, count)
+    up_all = lax.dynamic_slice_in_dim(up_four, group * group_slots, group_slots, 0)
+    two_mine = lax.dynamic_slice_in_dim(two_all, shard * slots_dev, slots_dev, 0)
+    two_four = lax.all_gather(two_mine, ("grp", "seq"), axis=0, tiled=True)
+    back_part, down_part, saved = feed(two_all, up_all, wide_t, down_weight)
+    layer_out = resid + lax.psum_scatter(
+        down_part, "seq", scatter_dimension=0, tiled=True
+    ).astype(jnp.float32)
+    resid_back, branch_all, sums = third(back_part, resid, upstream, norm_gains, count)
+    mix_part, mix_term, out_term, bias_term = attend_heads_back(
+        branch_all, normed_all, mix_t, out_weight, tables, lab_col, lab_row,
+        (query, key, value, attended, lse),
+    )
+    mix_sum, out_sum = lax.psum((mix_term, out_term), "grp")
+    bias_sum = lax.psum(bias_term, "grp")
+    tokens_grad, four = fourth(mix_part, tokens, resid_back, norm_gains, sums)
+    wide_grad, down_grad = grads(two_all, up_all, saved, two_four, up_four, wide_t, down_weight)
+    return (
+        layer_out.astype(jnp.bfloat16),
+        tokens_grad,
+        four[0:2],
+        four[2:4],
+        jnp.transpose(mix_sum, (1, 0, 2)).astype(jnp.float32),
+        bias_sum,
+        out_sum.astype(jnp.float32),
+        jnp.transpose(wide_grad, (2, 0, 1)),
         down_grad,
     )
 
@@ -326,7 +1110,7 @@
         P(("grp", "seq"), None),
     )
     return jax.shard_map(
-        on_device,
+        on_device if mesh.shape["seq"] == RING else plain_device,
         mesh=mesh,
         in_specs=placed,
         out_specs=(

time: 1250 us -> 528 us (0.42)
  waiting for transfers between devices: 879 us -> 87.5 us
  Pallas kernels: 0 us -> 364 us
  matrix products: 145 us -> 0 us
  blocking collectives: 92.4 us -> 16.2 us
  other arithmetic: 47.1 us -> 15.4 us
  local copies, waits for them, and re-layouts: 49.7 us -> 21.6 us
  starting transfers between devices: 13.4 us -> 0.38 us
    psum x1, waiting for transfers between devices: 407 us -> 24.4 us  [on_device(): mix_sum, out_sum = lax.psum((mix_term, out_term), 'grp')]
    pallas_call x0 -> x8, Pallas kernels: none -> 364 us  [the longest x4 198 us: call(): pl.pallas_call(kernel, out_shape=tuple((jax.ShapeDtypeStruct(*shape) for...]
    reduce_scatter x4 -> x1, waiting for transfers between devices: 233 us -> 47.1 us  [on_device(): lax.psum_scatter(down_part, 'seq', scatter_dimension=0, tiled=True)]
    all_gather x4 -> x2, waiting for transfers between devices: 183 us -> 15.9 us  [the longest x1 15.9 us: on_device(): up_four = lax.all_gather(upstream, ('grp', 'seq'), axis=0, tiled=True)]
    dot_general x26 -> x0, matrix products: 145 us -> none  [the longest x1 14.6 us: on_device(): jnp.einsum('tcf,dcf->td', mixin_back, mix_full, preferred_element_type=jn...]
    all_to_all x3 -> x0, waiting for transfers between devices: 54.7 us -> none  [the longest x1 35.6 us: on_device(): lax.all_to_all(sending.reshape(slots_dev, 3, seq_count, local_width), 'se...]
    psum x2 -> x1, blocking collectives: 52.5 us -> 16.2 us  [on_device(): bias_sum = lax.psum(bias_term, 'grp')]
    all_to_all x1 -> x0, blocking collectives: 29.5 us -> none  [on_device(): lax.all_to_all(lowered, 'seq', split_axis=0, concat_axis=2, tiled=True)]
  transfers between devices with their start and end apart: 13 -> 4, of which waited for: 10 -> 3; matrix products, arithmetic and copies ran while one was open for 15% -> 3% of each run, Pallas kernels for 0% -> 70%
where the time goes in v1:
time: 528 us; the launch traced here: 520 us
  Pallas kernels  364 us (69%)
  waiting for transfers between devices  87.5 us (17%)
  local copies, waits for them, and re-layouts  21.6 us (4%)
  blocking collectives  16.2 us (3%)
  other arithmetic  15.4 us (3%)
  between operations  14.7 us (3%)
    pallas_call x4, Pallas kernels, call(): pl.pallas_call(kernel, out_shape=tuple((jax.ShapeDtypeStruct(*shape) for...  198 us
    pallas_call x1, Pallas kernels, grads(): pl.pallas_call(grads_kernel, out_shape=(jax.ShapeDtypeStruct((2, local, w...  78.8 us
    reduce_scatter x1, waiting for transfers between devices, on_device(): lax.psum_scatter(down_part, 'seq', scatter_dimension=0, tiled=True)  47.1 us
    pallas_call x1, Pallas kernels, feed(): pl.pallas_call(feed_kernel, out_shape=(part, part, jax.ShapeDtypeStruct((...  33.3 us
    pallas_call x1, Pallas kernels, attend_heads_back(): pl.pallas_call(attend_back_kernel, out_shape=(jax.ShapeDtypeStruct((total...  30.7 us
    psum x1, waiting for transfers between devices, on_device(): mix_sum, out_sum = lax.psum((mix_term, out_term), 'grp')  24.4 us
    pallas_call x1, Pallas kernels, attend_heads(): pl.pallas_call(attend_kernel, out_shape=(slab, slab, slab, slab, jax.Shap...  23.2 us
    psum x1, blocking collectives, on_device(): bias_sum = lax.psum(bias_term, 'grp')  16.2 us
  transfers between devices with their start and end apart: 4, of which 3 were waited for; matrix products, arithmetic and copies ran while one was open for 3% of the time, Pallas kernels for 70%

profile of v1, /device:TPU:0, one launch (start us, length us, event | category | flops | bytes accessed | tf_op | source)
XLA Modules:
  0.0 519.9 jit_solution(11599170903143987648)
XLA Ops:
  7.2 0.0 copy-start
  7.2 0.0 copy-start.8
  7.2 0.0 copy-start.9
  7.2 0.0 all-gather.3.cloned.1.call-start
  7.3 1.4 select_reduce_fusion.3
  8.6 0.8 select_reduce_fusion.2
  9.4 0.7 add.60
  10.0 0.1 select_reduce_fusion.1
  10.1 0.7 broadcast_add_fusion
  10.8 0.0 copy-start.11
  10.8 0.1 dynamic-slice_compare_fusion
  10.9 1.9 broadcast_select_fusion.upstream
  12.8 0.0 all-gather.3.cloned.1.call-update
  12.9 0.0 all-gather.5.cloned.1.call-start
  12.9 0.7 convert_element_type.25.bias
  13.6 0.2 multiply_sine_fusion
  13.9 0.2 copy.26
  14.1 0.2 copy.25
  14.3 0.2 copy.28.lab_col
  14.6 0.0 copy-done
  14.6 0.0 copy-start.7
  14.6 0.0 copy-start.13
  14.6 27.7 %shard_map.178.normed_all = bf16[1024,2048]{1,0:T(8,128)(2,1)S(1)} custom-call(bf16[128,2048]{1,0:T(8,128)(2,1)S(1)} %copy-done, f32[2,2048]{1,0:T(2,128)S(1)} %copy-done.8, f32[2,2048]{1,0:T(2,128)S(1)} %copy-done.9), custom_call_target="tpu_custom_call" | custom-call | bytes 20000000 | tf_op jit(solution)/shard_map/pallas_call | solution.py:542
  42.3 0.0 copy-start.2
  42.3 2.0 copy-done.2
  44.4 0.1 broadcast_select_fusion.1
  44.5 0.1 pad_maximum_fusion.tables
  44.6 0.0 copy-start.6
  44.6 0.0 copy-done.11
  44.6 0.0 copy-done.7
  44.6 0.0 copy-done.13
  44.6 23.2 %shard_map.179 = (bf16[1024,256]{1,0:T(8,128)(2,1)S(1)}, bf16[1024,256]{1,0:T(8,128)(2,1)S(1)}, bf16[1024,256]{1,0:T(8,128)(2,1)S(1)}, bf16[1024,256]{1,0:T(8,12...) custom-call(bf16[1024,2048]{1,0:T(8,128)(2,1)} %copy-done.2, bf16[3,2048,256]{2,1,0:T(8,128)(2,1)} %bitcast.16, ...), custom_call_target="tpu_custom_call" | custom-call | flops 7516192768 | bytes 16777216 | tf_op jit(solution)/shard_map/pallas_call | solution.py:709
  67.8 0.6 copy-done.18
  68.4 0.0 copy-start.3
  68.4 2.9 copy-done.3
  71.4 70.8 %shard_map.180 = (f32[128,2048]{1,0:T(8,128)S(1)}, bf16[1024,2048]{1,0:T(8,128)(2,1)S(1)}) custom-call(bf16[1024,2048]{1,0:T(8,128)(2,1)S(1)} %copy-done.3, bf16[128,2048]{1,0:T(8,128)(2,1)S(1)} %copy-done, f32[2,2048]{1,0:T(2,128)S(1)} %copy-done.8, f32[2,2048]{1,0:T(2,128)S(1)} %copy-done.9), custom_call_target="tpu_custom_call" | custom-call | bytes 20000000 | tf_op jit(solution)/shard_map/pallas_call | solution.py:542
  142.3 2.0 copy-done.10
  144.2 0.8 constant_dynamic-slice_fusion
  145.1 0.0 all-gather.5.cloned.1.call-update
  145.1 0.3 all-reduce.3.cloned.1.call-start
  145.4 15.9 %all-gather.3.cloned.1.call-done.up_four = bf16[4096,2048]{1,0:T(8,128)(2,1)} async-done(((bf16[128,2048]{1,0:T(8,128)(2,1)}), bf16[4096,2048]{1,0:T(8,128)(2,1)}) %all-gather.3.cloned.1.call-update) | async-done | bytes 16777232 | tf_op jit(solution)/shard_map/all_gather | solution.py:1064
  161.3 4.7 constant_dynamic-slice_fusion.1.up_all
  166.0 33.3 %shard_map.181 = (bf16[1024,2048]{1,0:T(8,128)(2,1)}, bf16[1024,2048]{1,0:T(8,128)(2,1)}, bf16[3,704,1024]{2,1,0:T(8,128)(2,1)}) custom-call(bf16[1024,2048]{1,0:T(8,128)(2,1)} %copy-done.10, bf16[1024,2048]{1,0:T(8,128)(2,1)} %constant_dynamic-slice_fusion.1.up_all, bf16[2,704,2048]{2,1,0:T(8,128)(2,1)} %bitcast.14, bf16[704,2048]{1,0:T(8,128)(2,1)} %down_hbm.3), custom_call_target="tpu_custom_call" | custom-call | flops 19327352832 | bytes 41943040 | tf_op jit(solution)/shard_map/pallas_call | solution.py:905
  199.3 0.0 copy-start.5
  199.4 2.2 copy-done.5
  201.5 62.1 %shard_map.182 = (f32[128,2048]{1,0:T(8,128)S(1)}, bf16[1024,2048]{1,0:T(8,128)(2,1)S(1)}, f32[2,2048]{1,0:T(2,128)S(1)}) custom-call(bf16[1024,2048]{1,0:T(8,128)(2,1)S(1)} %copy-done.5, f32[128,2048]{1,0:T(8,128)S(1)} %get-tuple-element.36.resid, bf16[128,2048]{1,0:T(8,128)(2,1)S(1)} %copy-done.1, f32[2,2048]{1,0:T(2,128)S(1)} %copy-done.8), custom_call_target="tpu_custom_call" | custom-call | bytes 20000000 | tf_op jit(solution)/shard_map/pallas_call | solution.py:542
  263.7 0.0 copy-start.12
  263.7 2.0 copy-done.12
  265.7 30.7 %shard_map.183 = (bf16[1024,2048]{1,0:T(8,128)(2,1)}, bf16[3,2048,256]{2,1,0:T(8,128)(2,1)}, bf16[256,2048]{1,0:T(8,128)(2,1)}, f32[3,256]{1,0:T(4,128)}) custom-call(bf16[1024,2048]{1,0:T(8,128)(2,1)} %copy-done.12, bf16[1024,2048]{1,0:T(8,128)(2,1)} %copy-done.2, bf16[3,2048,256]{2,1,0:T(8,128)(2,1)} %bitcast.17, bf16[256,2048]{1,0:T(8,128)(2,1)} %out_weight.3, ...), custom_call_target="tpu_custom_call" | custom-call | flops 17179869184 | bytes 31457280 | tf_op jit(solution)/shard_map/pallas_call | solution.py:821
  296.4 0.0 copy-start.20
  296.4 0.0 all-reduce.3.cloned.1.call-update
  296.4 0.0 reduce-scatter.2.cloned.1.call-start
  296.5 2.2 copy-done.4
  298.7 37.4 %shard_map.184 = (bf16[128,2048]{1,0:T(8,128)(2,1)S(1)}, f32[4,2048]{1,0:T(4,128)S(1)}) custom-call(bf16[1024,2048]{1,0:T(8,128)(2,1)S(1)} %copy-done.4, bf16[128,2048]{1,0:T(8,128)(2,1)S(1)} %copy-done, f32[128,2048]{1,0:T(8,128)S(1)} %get-tuple-element.47.resid_back, f32[2,2048]{1,0:T(2,128)S(1)} %copy-done.8, f32[2,2048]{1,0:T(2,128)S(1)} %get-tuple-element.48.sums), custom_call_target="tpu_custom_call" | custom-call | bytes 20000000 | tf_op jit(solution)/shard_map/pallas_call | solution.py:542
  336.1 16.2 %psum.22 = f32[3,256]{1,0:T(4,128)} all-reduce(f32[3,256]{1,0:T(4,128)S(1)} %copy-done.20), channel_id=1, replica_groups=mesh['grp'=4,'seq'=8] {'grp'}, use_global_device_ids=true, to_apply=%region_6.7 | all-reduce | flops 768 | bytes 6144 | tf_op jit(solution)/shard_map/psum | solution.py:1082
  352.3 0.0 reduce-scatter.2.cloned.1.call-update
  352.3 0.6 fusion.3
  352.9 78.8 %shard_map.185 = (f32[2,704,2048]{2,1,0:T(8,128)}, f32[704,2048]{1,0:T(8,128)}) custom-call(bf16[1024,2048]{1,0:T(8,128)(2,1)} %copy-done.10, bf16[1024,2048]{1,0:T(8,128)(2,1)} %constant_dynamic-slice_fusion.1.up_all, bf16[3,704,1024]{2,1,0:T(8,128)(2,1)} %get-tuple-element.54.saved, bf16[4096,2048]{1,0:T(8,128)(2,1)} %all-gather.5.cloned.1.call-done.two_four, ...), custom_call_target="tpu_custom_call" | custom-call | flops 64424509440 | bytes 62914560 | tf_op jit(solution)/shard_map/pallas_call | solution.py:995
  431.8 24.4 %all-reduce.3.cloned.1.call-done = (bf16[2048,3,256]{2,0,1:T(8,128)(2,1)}, bf16[256,2048]{1,0:T(8,128)(2,1)}) async-done(((bf16[2048,3,256]{2,0,1:T(8,128)(2,1)}, bf16[256,2048]{1,0:T(8,128)(2,1)}), (bf16[2048,3,256]{2,0,1:T(8,128)(2,1)}, bf16[256,2048]{1,0:T(8,128)(2,1)})) %all-reduce.3.cloned.1.call-update) | async-done | bytes 4194320 | tf_op jit(solution)/shard_map/psum | solution.py:1081
  456.2 5.2 %convert_element_type.30 = f32[2048,3,256]{2,0,1:T(8,128)} convert(bf16[2048,3,256]{2,0,1:T(8,128)(2,1)} %get-tuple-element.59) | non-fusion elementwise | flops 1572864 | bytes 9437184 | tf_op jit(solution)/shard_map/convert_element_type | solution.py:1090
  461.4 1.6 convert_element_type.31
  462.9 47.1 %reduce-scatter.2.cloned.1.call-done = bf16[128,2048]{1,0:T(8,128)(2,1)} async-done(((bf16[1024,2048]{1,0:T(8,128)(2,1)}), bf16[128,2048]{1,0:T(8,128)(2,1)}) %reduce-scatter.2.cloned.1.call-update) | async-done | bytes 524304 | tf_op jit(solution)/shard_map/reduce_scatter | solution.py:1073
  510.1 1.9 add_convert_fusion
  512.0 0.8 copy.33
  (26 shorter events, 0.2 us)
Async XLA Ops:
  7.2 7.4 %copy-start = (bf16[128,2048]{1,0:T(8,128)(2,1)S(1)}, bf16[128,2048]{1,0:T(8,128)(2,1)}, u32[]{:S(2)}) copy-start(bf16[128,2048]{1,0:T(8,128)(2,1)} %tokens.5) | copy-start | bytes 1572868
  7.2 7.4 %copy-start.8 = (f32[2,2048]{1,0:T(2,128)S(1)}, f32[2,2048]{1,0:T(2,128)}, u32[]{:S(2)}) copy-start(f32[2,2048]{1,0:T(2,128)} %gains.7) | copy-start | bytes 49156
  7.2 7.4 %copy-start.9 = (f32[2,2048]{1,0:T(2,128)S(1)}, f32[2,2048]{1,0:T(2,128)}, u32[]{:S(2)}) copy-start(f32[2,2048]{1,0:T(2,128)} %biases.3) | copy-start | bytes 49156
  7.2 154.1 %all-gather.3.cloned.1.call-start = ((), (), s32[]{:S(2)}) async-start(), calls=%async_computation.1 | async-start | bytes 17301504 | tf_op jit(solution)/shard_map/all_gather | solution.py:1064
  10.8 33.8 %copy-start.11 = (s32[1024]{0:T(1024)}, s32[1024]{0:T(1024)S(1)}, u32[]{:S(2)}) copy-start(s32[1024]{0:T(1024)S(1)} %get-tuple-element.69) | copy-start | bytes 12292
  12.9 340.1 %all-gather.5.cloned.1.call-start = ((), (), s32[]{:S(2)}) async-start(), calls=%async_computation.3 | async-start | bytes 17301504 | tf_op jit(solution)/shard_map/all_gather | solution.py:1071
  14.6 30.0 %copy-start.7 = (s32[1024,1]{1,0:T(8,128)}, s32[1024,1]{1,0:T(8,128)S(1)}, u32[]{:S(2)}) copy-start(s32[1024,1]{1,0:T(8,128)S(1)} %copy.28.lab_col) | copy-start | bytes 12292
  14.6 30.0 %copy-start.13 = (bf16[256,2048]{1,0:T(8,128)(2,1)S(1)}, bf16[256,2048]{1,0:T(8,128)(2,1)}, u32[]{:S(2)}) copy-start(bf16[256,2048]{1,0:T(8,128)(2,1)} %out_weight.3) | copy-start | bytes 3145732
  42.3 2.0 copy-start.2
  44.6 23.2 %copy-start.6 = (f32[3,1024,128]{2,1,0:T(8,128)}, f32[3,1024,128]{2,1,0:T(8,128)S(1)}, u32[]{:S(2)}) copy-start(f32[3,1024,128]{2,1,0:T(8,128)S(1)} %pad_maximum_fusion.tables) | copy-start | bytes 4718596
  67.8 0.6 copy-start.18
  68.4 73.8 %copy-start.14 = (bf16[1024,256]{1,0:T(8,128)(2,1)}, bf16[1024,256]{1,0:T(8,128)(2,1)S(1)}, u32[]{:S(2)}) copy-start(bf16[1024,256]{1,0:T(8,128)(2,1)S(1)} %get-tuple-element.41.query) | copy-start | bytes 1572868
  68.4 73.8 %copy-start.15 = (bf16[1024,256]{1,0:T(8,128)(2,1)}, bf16[1024,256]{1,0:T(8,128)(2,1)S(1)}, u32[]{:S(2)}) copy-start(bf16[1024,256]{1,0:T(8,128)(2,1)S(1)} %get-tuple-element.42.key) | copy-start | bytes 1572868
  68.4 73.8 %copy-start.16 = (bf16[1024,256]{1,0:T(8,128)(2,1)}, bf16[1024,256]{1,0:T(8,128)(2,1)S(1)}, u32[]{:S(2)}) copy-start(bf16[1024,256]{1,0:T(8,128)(2,1)S(1)} %get-tuple-element.43.value) | copy-start | bytes 1572868
  68.4 73.8 %copy-start.17 = (bf16[1024,256]{1,0:T(8,128)(2,1)}, bf16[1024,256]{1,0:T(8,128)(2,1)S(1)}, u32[]{:S(2)}) copy-start(bf16[1024,256]{1,0:T(8,128)(2,1)S(1)} %get-tuple-element.44.attended) | copy-start | bytes 1572868
  68.4 2.9 copy-start.3
  142.2 2.0 copy-start.10
  145.1 311.1 %all-reduce.3.cloned.1.call-start = ((), (), s32[]{:S(2)}) async-start(), calls=%async_computation.4 | async-start | bytes 8388608 | tf_op jit(solution)/shard_map/psum | solution.py:1081
  166.0 33.3 %copy-start.1 = (bf16[128,2048]{1,0:T(8,128)(2,1)S(1)}, bf16[128,2048]{1,0:T(8,128)(2,1)}, u32[]{:S(2)}) copy-start(bf16[128,2048]{1,0:T(8,128)(2,1)} %broadcast_select_fusion.upstream) | copy-start | bytes 1572868
  199.3 2.2 copy-start.5
  263.7 2.0 copy-start.12
  296.4 39.7 %copy-start.20 = (f32[3,256]{1,0:T(4,128)S(1)}, f32[3,256]{1,0:T(4,128)}, u32[]{:S(2)}) copy-start(f32[3,256]{1,0:T(4,128)} %get-tuple-element.52) | copy-start | bytes 9220
  296.4 213.7 %reduce-scatter.2.cloned.1.call-start = ((), (), s32[]{:S(2)}) async-start(), calls=%async_computation.2 | async-start | bytes 4718592 | tf_op jit(solution)/shard_map/reduce_scatter | solution.py:1073
  296.5 2.2 copy-start.4
  456.2 5.2 %copy-start.19 = (bf16[256,2048]{1,0:T(8,128)(2,1)S(1)}, bf16[256,2048]{1,0:T(8,128)(2,1)}, u32[]{:S(2)}) copy-start(bf16[256,2048]{1,0:T(8,128)(2,1)} %get-tuple-element.60) | copy-start | bytes 3145732
Sparse Core Ops, SparseCore 0:
  13.0 148.2 all-gather.2
  164.1 132.8 all-gather.4
  299.5 156.5 all-reduce.2
  459.7 50.3 reduce-scatter.1
